TPU v7x, 32 devices: a whole 2x2x4 slice. The times are simulated.
32 devices in a mesh: scen: 2 (over x), row: 4 (over y, core), col: 4 (over z).
Axes of the slice: x: 2, y: 2, z: 4, core: 2. Of those that a mesh axis runs over, the one named last changes fastest.
Arguments:
- root_matrix: float32 [8192, 8192], P(('scen', 'row'), 'col'), may hold values from -1 to 32, as said below
- inverse_block: bfloat16 [32, 1024, 1024], P(('scen', 'row', 'col')), may hold values from -0.05 to 3, as said below
- link_tiles: bfloat16 [32, 20, 1024, 128], P(('scen', 'row', 'col')), may hold values from -0.1875 to 0.1875
- tile_mask: int32 [32, 64], P(('scen', 'row', 'col')), may hold values from 0 to 1, as said below
- panel_index: int32 [1], replicated, may hold values from 0 to 31
Outputs:
- trailing: float32 [8192, 8192], P(('scen', 'row'), 'col')
- factor: float32 [8192, 128], P(('scen', 'row', 'col'))
Inputs may be any that keep to these rules, and one draw needn't show every extreme that they name: `root_matrix`: Symmetric, with the diagonal between 8 and 32 and every other entry of magnitude under 1. `inverse_block`: each block is symmetric positive definite, its diagonal between 1 and 3. `tile_mask`: each scenario flags between 4 and 20 tiles, at most 4 among each aligned group of 8 tiles (tiles 0 to 7, and so on); some scenario flags exactly 20 tiles, 4 in each of its first groups.
All inputs are finite; a program needn't handle non-finite values.
Results may differ from a plain program's by a relative error of at most 0.00049.
Values may be sent and summed in bfloat16 or wider, within the bound.
A program may use at most 64 MiB of HBM per device.

v0:
```python
import jax
import jax.numpy as jnp
from jax import lax
from jax.sharding import PartitionSpec as P

PANEL = 128


def broadcast(block, axis, source):
    block = jnp.where(lax.axis_index(axis) == source, block, jnp.zeros_like(block))
    return lax.psum(block, axis)


def select_matrix(tile_flags, slot_count):
    slot_order = jnp.cumsum(tile_flags) - 1
    slot_ids = lax.broadcasted_iota(jnp.int32, (slot_count, tile_flags.shape[0]), 0)
    hit = (slot_order[None, :] == slot_ids) & (tile_flags[None, :] == 1)
    return jnp.where(hit, jnp.float32(1.0), jnp.float32(0.0))


def compact_term(inverse, tiles_here, tile_flags, panel_at):
    slot_count, inner_rows, tile_rows = tiles_here.shape
    selector = select_matrix(tile_flags, slot_count)
    per_panel = PANEL // tile_rows
    picked = lax.dynamic_slice_in_dim(selector, panel_at * per_panel, per_panel, 1)
    columns = jnp.einsum(
        "kj,knt->njt", picked.astype(jnp.bfloat16), tiles_here, preferred_element_type=jnp.float32
    )
    columns = columns.reshape(inner_rows, PANEL).astype(jnp.bfloat16)
    weighted = jnp.dot(inverse, columns, preferred_element_type=jnp.float32).astype(jnp.bfloat16)
    product = jnp.einsum("knt,na->kta", tiles_here, weighted, preferred_element_type=jnp.float32)
    return (selector, product)


def dense_term(selector, product, base_cols, base_start):
    spread = jnp.einsum("kr,kta->rta", selector, product, precision=lax.Precision.HIGHEST)
    scenario = spread.reshape(selector.shape[1] * product.shape[1], PANEL)
    own_block = lax.dynamic_slice_in_dim(scenario, base_start, base_cols.shape[0], 0) + base_cols
    return lax.dynamic_update_slice_in_dim(scenario, own_block, base_start, 0)


def lower_rows(diagonal, rows_here, first_row, first_col):
    chol_lower = jnp.linalg.cholesky(diagonal)
    solved = jax.scipy.linalg.solve_triangular(chol_lower, rows_here.T, lower=True).T
    row_ids = first_row + lax.broadcasted_iota(jnp.int32, (rows_here.shape[0], 1), 0)
    return jnp.where(row_ids >= first_col, solved, 0.0)


def trailing_rows(factor_part, first_row, first_col):
    rounded = factor_part.astype(jnp.bfloat16)
    row_ids = first_row + lax.broadcasted_iota(jnp.int32, (factor_part.shape[0], 1), 0)
    return jnp.where(row_ids >= first_col + PANEL, rounded, jnp.zeros_like(rounded))


def local(root_matrix, inverse_block, link_tiles, tile_mask, panel_index):
    panel_at = panel_index[0]
    tile_flags = tile_mask[0]
    selector, product = compact_term(inverse_block[0], link_tiles[0], tile_flags, panel_at)
    tile_count = selector.shape[1]
    tile_rows = product.shape[1]
    total_rows = tile_count * tile_rows
    row_block, col_block = root_matrix.shape
    scen_at = lax.axis_index("scen")
    row_at = lax.axis_index("row")
    col_at = lax.axis_index("col")
    row_count = lax.axis_size("row")
    col_count = lax.axis_size("col")
    scen_count = lax.axis_size("scen")
    block_at = scen_at * row_count + row_at
    first_col = panel_at * PANEL
    owner_col = first_col // col_block
    base_cols = lax.dynamic_slice_in_dim(root_matrix, first_col - owner_col * col_block, PANEL, 1)
    base_cols = jnp.where(col_at == owner_col, base_cols, 0.0)
    piece_rows = row_block // col_count
    scenario = dense_term(selector, product, base_cols, block_at * row_block)
    slab_rows = total_rows // scen_count
    slab_sum = lax.psum_scatter(scenario, "scen", scatter_dimension=0, tiled=True)
    slab_sum = lax.psum(slab_sum, ("row", "col"))
    owner_slab = first_col // slab_rows
    diag_part = lax.dynamic_slice_in_dim(slab_sum, first_col - owner_slab * slab_rows, PANEL, 0)
    diagonal = broadcast(diag_part, "scen", owner_slab)
    slab_first = scen_at * slab_rows
    slab_factor = lower_rows(diagonal, slab_sum, slab_first, first_col)
    factor_rows = lax.dynamic_slice_in_dim(
        slab_factor, (row_at * col_count + col_at) * piece_rows, piece_rows, 0
    )
    ending = trailing_rows(slab_factor, slab_first, first_col)
    all_factor = lax.all_gather(ending, "scen", axis=0, tiled=True)
    own_rows = lax.dynamic_slice_in_dim(all_factor, block_at * row_block, row_block, 0)
    own_cols = lax.dynamic_slice_in_dim(all_factor, col_at * col_block, col_block, 0)
    update = lax.dot_general(
        own_rows, own_cols, (((1,), (1,)), ((), ())), preferred_element_type=jnp.float32
    )
    return (root_matrix - update, factor_rows)


def solution(mesh):
    in_specs = (
        P(("scen", "row"), "col"),
        P(("scen", "row", "col"), None, None),
        P(("scen", "row", "col"), None, None, None),
        P(("scen", "row", "col"), None),
        P(),
    )
    out_specs = (P(("scen", "row"), "col"), P(("scen", "row", "col"), None))
    return jax.shard_map(local, mesh=mesh, in_specs=in_specs, out_specs=out_specs, check_vma=False)
```

profile of v0, /device:TPU:7, one launch (start us, length us, event | category | flops | bytes accessed | tf_op | source)
XLA Modules:
  0.0 293.4 jit_solution(16068640463012025839)
XLA Ops:
  7.2 0.0 copy-start
  7.2 0.0 reduce-scatter.2.cloned.1.call-start
  8.1 0.7 compare_bitcast_fusion
  8.7 0.7 copy.11
  9.5 0.1 reduce-window.8
  9.6 0.1 add_reduce_fusion
  9.7 0.1 fusion.24
  9.8 7.5 %fusion = f32[1,1024,128]{2,0,1:T(1,128)} fusion(bf16[20,1024,128]{2,1,0:T(8,128)(2,1)} %bitcast.50, bf16[20,64]{0,1:T(8,128)(2,1)S(1)} %fusion.24, s32[]{:T(128)S(6)} %select_n.61), kind=kOutput, calls=%fused_computation | convolution fusion | flops 5242880 | bytes 5767684 | tf_op jit(solution)/shard_map/kj,knt->njt/dot_general | solution.py:26
  17.2 0.0 copy-done
  17.3 4.2 %fusion.13 = f32[128,20,128]{2,0,1:T(8,128)S(1)} fusion(bf16[1,1024,1024]{2,1,0:T(8,128)(2,1)S(1)} %copy-done, f32[1024,128]{1,0:T(8,128)} %bitcast.52, bf16[1,20,1024,128]{3,2,1,0:T(8,128)(2,1)} %param.7), kind=kOutput, calls=%fused_computation.11 | convolution fusion | flops 939786240 | bytes 9175040 | tf_op jit(solution)/shard_map/knt,na->kta/dot_general | solution.py:31
  21.4 1.6 copy.17
  23.1 4.9 %fusion.4 = f32[64,128,128]{2,0,1:T(8,128)S(1)} fusion(f32[128,20,128]{0,1,2:T(8,128)} %copy.17, s32[64]{0:T(128)S(1)} %add_reduce_fusion, pred[64]{0:T(512)(128)(4,1)S(1)} %compare_bitcast_fusion), kind=kOutput, calls=%fused_computation.6 | convolution fusion | flops 251662080 | bytes 5505344 | tf_op jit(solution)/shard_map/kr,kta->rta/dot_general | solution.py:36
  27.9 4.4 %copy.13 = f32[64,128,128]{2,1,0:T(8,128)} copy(f32[64,128,128]{2,0,1:T(8,128)S(1)} %fusion.4) | data formatting | bytes 8388608 | tf_op jit(solution)/shard_map/kr,kta->rta/dot_general | solution.py:36
  32.4 2.0 add_dynamic-update-slice_fusion
  34.4 0.0 reduce-scatter.2.cloned.1.call-update
  34.5 0.0 all-reduce.3.cloned.1.call-start
  34.5 54.7 %reduce-scatter.2.cloned.1.call-done = f32[4096,128]{1,0:T(8,128)} async-done(((f32[8192,128]{1,0:T(8,128)}), f32[4096,128]{1,0:T(8,128)}) %reduce-scatter.2.cloned.1.call-update) | async-done | bytes 2097168 | tf_op jit(solution)/shard_map/reduce_scatter | solution.py:77
  89.2 0.0 all-reduce.3.cloned.1.call-update
  89.2 0.0 all-reduce.5.cloned.1.call-start
  89.3 100.8 %all-reduce.3.cloned.1.call-done = f32[4096,128]{1,0:T(8,128)} async-done(((f32[4096,128]{1,0:T(8,128)}), f32[4096,128]{1,0:T(8,128)}) %all-reduce.3.cloned.1.call-update) | async-done | bytes 2097168 | tf_op jit(solution)/shard_map/psum | solution.py:78
  190.2 1.5 dynamic-slice_select_fusion
  191.6 0.0 all-reduce.5.cloned.1.call-update
  191.6 0.2 all-gather.2.cloned.1.call-start
  191.9 21.5 %all-reduce.5.cloned.1.call-done = f32[128,128]{1,0:T(8,128)} async-done(((f32[128,128]{1,0:T(8,128)}), f32[128,128]{1,0:T(8,128)}) %all-reduce.5.cloned.1.call-update) | async-done | bytes 65552 | tf_op jit(solution)/shard_map/psum | solution.py:11
  213.4 0.9 copy.14
  214.3 0.9 fusion.21
  215.2 11.7 %cholesky.15 = f32[128,128]{1,0:T(8,128)S(1)} custom-call(f32[128,128]{1,0:T(8,128)S(1)} %fusion.21), custom_call_target="Cholesky" | custom-call | tf_op jit(solution)/shard_map/jit(cholesky)/cholesky | solution.py:43
  226.9 0.6 compare_reduce_fusion
  227.6 0.7 fusion.19
  228.3 9.8 %custom-call.7 = f32[1,128,128]{1,2,0:T(8,128)S(1)} custom-call(f32[1,128,128]{2,1,0:T(8,128)S(1)} %fusion.19), custom_call_target="InvertDiagBlocksLowerTriangular" | custom-call | tf_op jit(solution)/shard_map/jit(_solve_triangular)/triangular_solve | solution.py:44
  238.1 6.8 %convert_select_fusion = (bf16[4096,128]{1,0:T(8,128)(2,1)}, f32[4096,128]{1,0:T(8,128)}) fusion(pred[4096]{0:T(1024)(128)(4,1)S(1)} %fusion.26, f32[4096,128]{1,0:T(8,128)} %all-reduce.3.cloned.1.call-done, f32[1,128,128]{1,2,0:T(8,128)S(1)} %custom-call.7, pred[4096]{0:T(1024)(128)(4,1)S(1)} %fusion.25), kind=kOutput, calls=%fused_computation.10 | convolution fusion | flops 806879232 | bytes 5316608 | tf_op jit(solution)/shard_map/jit(_solve_triangular)/triangular_solve | solution.py:44
  244.9 0.0 all-gather.2.cloned.1.call-update
  244.9 1.6 constant_dynamic-slice_fusion
  246.5 32.1 %all-gather.2.cloned.1.call-done = bf16[8192,128]{1,0:T(8,128)(2,1)} async-done(((bf16[4096,128]{1,0:T(8,128)(2,1)}), bf16[8192,128]{1,0:T(8,128)(2,1)}) %all-gather.2.cloned.1.call-update) | async-done | bytes 2097168 | tf_op jit(solution)/shard_map/all_gather | solution.py:88
  278.6 8.3 %convolution_subtract_fusion = f32[1024,2048]{1,0:T(8,128)} fusion(f32[1024,2048]{1,0:T(8,128)} %param.5, bf16[8192,128]{1,0:T(8,128)(2,1)} %all-gather.2.cloned.1.call-done, s32[]{:T(128)S(6)} %select_n.74, s32[]{:T(128)S(6)} %select_n.62), kind=kOutput, calls=%fused_computation.3 | convolution fusion | flops 538968064 | bytes 17563656 | tf_op jit(solution)/shard_map/dot_general | solution.py:91
  (3 shorter events, 0.1 us)
Async XLA Ops:
  7.2 10.1 %copy-start = (bf16[1,1024,1024]{2,1,0:T(8,128)(2,1)S(1)}, bf16[1,1024,1024]{2,1,0:T(8,128)(2,1)}, u32[]{:S(2)}) copy-start(bf16[1,1024,1024]{2,1,0:T(8,128)(2,1)} %param.6) | copy-start | bytes 6291460
  7.2 82.0 %reduce-scatter.2.cloned.1.call-start = ((), (), s32[]{:S(2)}) async-start(), calls=%async_computation.1 | async-start | bytes 6291456 | tf_op jit(solution)/shard_map/reduce_scatter | solution.py:77
  34.5 155.7 %all-reduce.3.cloned.1.call-start = ((), (), s32[]{:S(2)}) async-start(), calls=%async_computation.2 | async-start | bytes 4194304 | tf_op jit(solution)/shard_map/psum | solution.py:78
  89.2 124.2 %all-reduce.5.cloned.1.call-start = ((), (), s32[]{:S(2)}) async-start(), calls=%async_computation.3 | async-start | bytes 131072 | tf_op jit(solution)/shard_map/psum | solution.py:11
  191.6 87.0 %all-gather.2.cloned.1.call-start = ((), (), s32[]{:S(2)}) async-start(), calls=%async_computation.4 | async-start | bytes 3145728 | tf_op jit(solution)/shard_map/all_gather | solution.py:88
Sparse Core Ops, SparseCore 0:
  34.6 54.5 reduce-scatter.1
  93.2 96.9 all-reduce.2
  193.0 20.3 all-reduce.4
  245.0 33.5 all-gather.1
where the time goes:
time: 296 us; the launch traced here: 293 us
  waiting for transfers between devices  209 us (71%)
  matrix products  31.7 us (11%)
  other arithmetic  28.2 us (10%)
  between operations  14.7 us (5%)
  local copies, waits for them, and re-layouts  9.31 us (3%)
    psum x1, waiting for transfers between devices, local(): slab_sum = lax.psum(slab_sum, ('row', 'col'))  101 us
    reduce_scatter x1, waiting for transfers between devices, local(): lax.psum_scatter(scenario, 'scen', scatter_dimension=0, tiled=True)  54.7 us
    all_gather x1, waiting for transfers between devices, local(): all_factor = lax.all_gather(ending, 'scen', axis=0, tiled=True)  32.1 us
    psum x1, waiting for transfers between devices, broadcast(): return lax.psum(block, axis)  21.5 us
    another operation x3, other arithmetic, lower_rows(): chol_lower = jnp.linalg.cholesky(diagonal)  12.4 us
    another operation x2, other arithmetic, lower_rows(): jax.scipy.linalg.solve_triangular(chol_lower, rows_here.T, lower=True)  10.5 us
    dot_general x1, matrix products, local(): lax.dot_general(own_rows, own_cols, (((1,), (1,)), ((), ())), preferred_e...  8.3 us
    dot_general x1, matrix products, compact_term(): jnp.einsum('kj,knt->njt', picked.astype(jnp.bfloat16), tiles_here, prefer...  7.47 us
  transfers between devices with their start and end apart: 4, of which 4 were waited for; matrix products, arithmetic and copies ran while one was open for 1% of the time, Pallas kernels for 0%

commit v1 on v0

--- a/solution.py
+++ b/solution.py
@@ -1,6 +1,8 @@
 import jax
 import jax.numpy as jnp
 from jax import lax
+from jax.experimental import pallas as pl
+from jax.experimental.pallas import tpu as pltpu
 from jax.sharding import PartitionSpec as P
 
 PANEL = 128
@@ -94,6 +96,371 @@
     return (root_matrix - update, factor_rows)
 
 
+MESH_ID = pl.DeviceIdType.MESH
+F32 = jnp.float32
+BF16 = jnp.bfloat16
+
+
+def term_kernel(panel_ref, mask_ref, inv_hbm, tiles_hbm, root_ref, out_ref, diag_ref, inv, tiles, left, sems):
+    slots = tiles.shape[0]
+    f = panel_ref[0]
+    scen_at, row_at, col_at = (lax.axis_index(a) for a in ("scen", "row", "col"))
+    group = scen_at * lax.axis_size("row") + row_at
+    inv_copy = pltpu.make_async_copy(inv_hbm, inv, sems.at[slots])
+    inv_copy.start()
+
+    def tile_copy(k):
+        return pltpu.make_async_copy(tiles_hbm.at[k], tiles.at[k], sems.at[k])
+
+    tile_total = mask_ref.shape[1]
+    before = lax.fori_loop(0, f, lambda t, n: n + mask_ref[0, t], 0)
+    total = lax.fori_loop(f, tile_total, lambda t, n: n + mask_ref[0, t], before)
+    linked = mask_ref[0, f]
+    first = jnp.minimum(before, slots - 1)
+    panel_copy = pltpu.make_async_copy(tiles_hbm.at[first], left, sems.at[slots + 1])
+    panel_copy.start()
+
+    @pl.loop(0, total)
+    def _(k):
+        tile_copy(k).start()
+
+    panel_copy.wait()
+    columns = jnp.where(linked == 1, left[...], jnp.zeros_like(left))
+    inv_copy.wait()
+    weighted = lax.dot_general(
+        columns, inv[...], (((0,), (0,)), ((), ())), preferred_element_type=F32
+    ).astype(BF16)
+
+    def one(t, at):
+        flag = mask_ref[0, t]
+
+        @pl.when(flag == 1)
+        def _():
+            tile_copy(at).wait()
+            out_ref[t] = jnp.dot(weighted, tiles[at], preferred_element_type=F32)
+
+        @pl.when(flag != 1)
+        def _():
+            out_ref[t] = jnp.zeros(out_ref.shape[1:], F32)
+
+        return at + flag
+
+    lax.fori_loop(0, tile_total, one, 0)
+    own_tiles = root_ref.shape[0] // PANEL
+
+    @pl.when(col_at == f // (tile_total // lax.axis_size("col")))
+    def _():
+        for i in range(own_tiles):
+            at = group * own_tiles + i
+            out_ref[at] = out_ref[at] + root_ref[i * PANEL : (i + 1) * PANEL, :].T
+
+    diag_ref[...] = out_ref[f]
+
+
+def scenario_tiles(root_matrix, inverse, tiles, tile_mask, panel_index):
+    slots, inner, tile_rows = tiles.shape
+    tile_total = tile_mask.shape[1]
+    own_rows, own_cols = root_matrix.shape
+    wide = own_cols // PANEL
+    return pl.pallas_call(
+        term_kernel,
+        out_shape=(
+            jax.ShapeDtypeStruct((tile_total, PANEL, tile_rows), F32),
+            jax.ShapeDtypeStruct((PANEL, PANEL), F32),
+        ),
+        grid_spec=pltpu.PrefetchScalarGridSpec(
+            num_scalar_prefetch=2,
+            grid=(1,),
+            in_specs=[
+                pl.BlockSpec(memory_space=pl.ANY),
+                pl.BlockSpec(memory_space=pl.ANY),
+                pl.BlockSpec((own_rows, PANEL), lambda i, p, m: (0, lax.rem(p[0], wide))),
+            ],
+            out_specs=[
+                pl.BlockSpec((tile_total, PANEL, tile_rows), lambda i, p, m: (0, 0, 0)),
+                pl.BlockSpec((PANEL, PANEL), lambda i, p, m: (0, 0)),
+            ],
+            scratch_shapes=[
+                pltpu.VMEM(inverse.shape, BF16),
+                pltpu.VMEM(tiles.shape, BF16),
+                pltpu.VMEM((inner, tile_rows), BF16),
+                pltpu.SemaphoreType.DMA((slots + 2,)),
+            ],
+        ),
+        compiler_params=pltpu.CompilerParams(vmem_limit_bytes=40 * 2**20),
+        name="scenario_tiles",
+    )(panel_index, tile_mask, inverse, tiles, root_matrix)
+
+
+def remote(src, dst, send, recv, device):
+    return pltpu.make_async_remote_copy(
+        src_ref=src, dst_ref=dst, send_sem=send, recv_sem=recv, device_id=device, device_id_type=MESH_ID
+    )
+
+
+def sum_kernel(tiles_hbm, diag_in, piece_ref, diag_ref, own, got0, got1, got2, acc, got3, got4,
+               dsum, dgot, dpart, dparts, send, recv, local_sem, dsend, drecv):
+    s, r, c = (lax.axis_index(a) for a in ("scen", "row", "col"))
+    y, k = r // 2, lax.rem(r, 2)
+    core = (s, 2 * y + 1 - k, c)
+    x_to = (1 - s, r, c)
+    y_to = (s, 2 * (1 - y) + k, c)
+    z1 = c + 1 - 2 * lax.rem(c, 2)
+    z2 = lax.rem(c + 2, 4)
+    me = s * 8 + y * 4 + c
+
+    def chip(o):
+        q = lax.rem(me + o, 16)
+        return q, (q // 8, 2 * lax.rem(q // 4, 2) + k, lax.rem(q, 4))
+
+    barrier = pltpu.get_barrier_semaphore()
+    pl.semaphore_signal(barrier, inc=1, device_id=core, device_id_type=MESH_ID)
+    for o in range(1, 16):
+        pl.semaphore_signal(barrier, inc=1, device_id=chip(o)[1], device_id_type=MESH_ID)
+    pl.semaphore_wait(barrier, 16)
+
+    core_diag = remote(diag_in, dgot, dsend.at[0], drecv.at[0], core)
+    core_diag.start()
+    core_copy = []
+    loads = []
+    for sp in range(2):
+        for yp in range(2):
+            i = sp * 2 + yp
+            cp = remote(tiles_hbm.at[pl.ds((i * 2 + 1 - k) * 8, 8)], got0.at[i], send.at[i], recv.at[i], core)
+            cp.start()
+            core_copy.append(cp)
+            ld = pltpu.make_async_copy(tiles_hbm.at[pl.ds((i * 2 + k) * 8, 8)], own.at[i], local_sem.at[i])
+            ld.start()
+            loads.append(ld)
+    core_diag.wait()
+    dsum[...] = diag_in[...] + dgot[...]
+    out1 = []
+    for o in range(1, 16):
+        q, dev = chip(o)
+        cp = remote(dsum.at[pl.ds(pl.multiple_of(q * 8, 8), 8)], dparts.at[o], dsend.at[o], drecv.at[o], dev)
+        cp.start()
+        out1.append(cp)
+    for i in range(4):
+        loads[i].wait()
+        core_copy[i].wait()
+        own[i] = own[i] + got0[i]
+    order = []
+    ax = []
+    for step in range(2):
+        yy = (1 - y) if step == 0 else y
+        ss = (1 - s) if step == 0 else s
+        a = remote(own.at[(1 - s) * 2 + yy, pl.ds(0, 4)], got1.at[0, step], send.at[4 + step], recv.at[4 + step], x_to)
+        b = remote(own.at[ss * 2 + 1 - y, pl.ds(4, 4)], got1.at[1, step], send.at[6 + step], recv.at[6 + step], y_to)
+        a.start()
+        b.start()
+        ax.append((a, b))
+    for cp in out1:
+        cp.wait_recv()
+    total = dsum[pl.ds(pl.multiple_of(me * 8, 8), 8), :]
+    for o in range(1, 16):
+        total = total + dparts[o]
+    dpart[...] = total
+    diag_ref[pl.ds(pl.multiple_of(me * 8, 8), 8), :] = total
+    out2 = []
+    for o in range(1, 16):
+        q, dev = chip(o)
+        cp = remote(dpart, diag_ref.at[pl.ds(pl.multiple_of(me * 8, 8), 8)], dsend.at[15 + o], drecv.at[15 + o], dev)
+        cp.start()
+        out2.append(cp)
+    ax[0][0].wait_recv()
+    acc[0, 0] = own[s * 2 + 1 - y, 0:4] + got1[0, 0]
+    a2 = remote(acc.at[0, 0], got2.at[0], send.at[8], recv.at[8], y_to)
+    a2.start()
+    ax[0][1].wait_recv()
+    acc[0, 1] = own[(1 - s) * 2 + y, 4:8] + got1[1, 0]
+    b2 = remote(acc.at[0, 1], got2.at[1], send.at[9], recv.at[9], x_to)
+    b2.start()
+    ax[1][0].wait_recv()
+    acc[1, 0] = own[s * 2 + y, 0:4] + got1[0, 1]
+    ax[1][1].wait_recv()
+    acc[1, 1] = own[s * 2 + y, 4:8] + got1[1, 1]
+    a2.wait_recv()
+    acc[1, 0] = acc[1, 0] + got2[0]
+    b2.wait_recv()
+    acc[1, 1] = acc[1, 1] + got2[1]
+    par = lax.rem(c, 2)
+    hi = c // 2
+    z_out = []
+    for h in range(2):
+        cp = remote(acc.at[1, h, pl.ds((1 - par) * 2, 2)], got3.at[h], send.at[10 + h], recv.at[10 + h], (s, r, z1))
+        cp.start()
+        z_out.append(cp)
+    z_out[0].wait_recv()
+    z_out[1].wait_recv()
+    a2.wait_send()
+    acc[0, 0, pl.ds(0, 2)] = acc[1, 1 - hi, pl.ds(par * 2, 2)] + got3[1 - hi]
+    last = remote(acc.at[0, 0, pl.ds(0, 2)], got4, send.at[12], recv.at[12], (s, r, z2))
+    last.start()
+    mine = acc[1, hi, pl.ds(par * 2, 2)] + got3[hi]
+    last.wait_recv()
+    piece_ref[...] = mine + got4[...]
+    for cp in out2:
+        cp.wait_recv()
+    for cp in out1 + out2 + [ax[0][0], ax[0][1], ax[1][0], ax[1][1], b2, *z_out, last]:
+        cp.wait_send()
+
+
+def reduced(tiles, diag):
+    tile = tiles.shape[1:]
+    vmem = pl.BlockSpec(memory_space=pltpu.VMEM)
+    return pl.pallas_call(
+        sum_kernel,
+        out_shape=(jax.ShapeDtypeStruct((2, *tile), F32), jax.ShapeDtypeStruct((PANEL, PANEL), F32)),
+        in_specs=[pl.BlockSpec(memory_space=pl.ANY), vmem],
+        out_specs=(vmem, vmem),
+        scratch_shapes=[
+            pltpu.VMEM((4, 8, *tile), F32),
+            pltpu.VMEM((4, 8, *tile), F32),
+            pltpu.VMEM((2, 2, 4, *tile), F32),
+            pltpu.VMEM((2, 4, *tile), F32),
+            pltpu.VMEM((2, 2, 4, *tile), F32),
+            pltpu.VMEM((2, 2, *tile), F32),
+            pltpu.VMEM((2, *tile), F32),
+            pltpu.VMEM(tile, F32),
+            pltpu.VMEM(tile, F32),
+            pltpu.VMEM((8, PANEL), F32),
+            pltpu.VMEM((16, 8, PANEL), F32),
+            pltpu.SemaphoreType.DMA((13,)),
+            pltpu.SemaphoreType.DMA((13,)),
+            pltpu.SemaphoreType.DMA((4,)),
+            pltpu.SemaphoreType.DMA((31,)),
+            pltpu.SemaphoreType.DMA((31,)),
+        ],
+        compiler_params=pltpu.CompilerParams(collective_id=0, has_side_effects=True, vmem_limit_bytes=32 * 2**20),
+        name="panel_sum",
+    )(tiles, diag)
+
+
+def gather_kernel(panel_ref, piece_ref, inv_ref, factor_ref, rows_ref, cols_ref, ending, send, recv, local_sem):
+    s, r, c = (lax.axis_index(a) for a in ("scen", "row", "col"))
+    y, k = r // 2, lax.rem(r, 2)
+    rows = factor_ref.shape[0]
+    to_col = 2 * s + y
+    is_self = to_col == c
+    barrier = pltpu.get_barrier_semaphore()
+    for o in range(1, 4):
+        pl.semaphore_signal(barrier, inc=1, device_id=(s, r, lax.rem(c + o, 4)), device_id_type=MESH_ID)
+    for kk in range(2):
+        for zz in range(4):
+            src = (c // 2, 2 * lax.rem(c, 2) + kk, zz)
+
+            @pl.when(jnp.logical_not(jnp.logical_and(is_self, jnp.logical_and(kk == k, zz == c))))
+            def _():
+                pl.semaphore_signal(barrier, inc=1, device_id=src, device_id_type=MESH_ID)
+
+    f = panel_ref[0]
+    first = (s * 4 + r) * (4 * rows) + c * rows
+    for i in range(2):
+        part = lax.dot_general(
+            piece_ref[i], inv_ref[...], (((0,), (1,)), ((), ())),
+            preferred_element_type=F32, precision=lax.Precision.HIGHEST,
+        )
+        ids = first + i * PANEL + lax.broadcasted_iota(jnp.int32, part.shape, 0)
+        factor_ref[i * PANEL : (i + 1) * PANEL, :] = jnp.where(ids >= f * PANEL, part, 0.0)
+        ending[i * PANEL : (i + 1) * PANEL, :] = jnp.where(ids >= f * PANEL + PANEL, part, 0.0).astype(BF16)
+
+    pl.semaphore_wait(barrier, jnp.where(is_self, 10, 11))
+
+    my_row = pl.ds(pl.multiple_of(c * rows, rows), rows)
+    my_slot = k * 4 + c
+    my_col = pl.ds(pl.multiple_of(my_slot * rows, rows), rows)
+    sends = []
+    n = 0
+    for ds_ in range(2):
+        for dr in range(4):
+            dev = (lax.rem(s + 1 - ds_, 2), lax.rem(r + 3 - dr, 4), to_col)
+            cp = remote(ending, cols_ref.at[my_col], send.at[n], recv.at[my_slot], dev)
+            n += 1
+            if ds_ == 1 and dr == 3:
+                self_cp = cp
+            else:
+                cp.start()
+                sends.append(cp)
+
+    @pl.when(jnp.logical_not(is_self))
+    def _():
+        self_cp.start()
+
+    for o in range(1, 4):
+        cp = remote(ending, rows_ref.at[my_row], send.at[n], recv.at[7 + o], (s, r, lax.rem(c + o, 4)))
+        cp.start()
+        n += 1
+        sends.append(cp)
+    own_row = pltpu.make_async_copy(ending, rows_ref.at[my_row], local_sem.at[0])
+    own_row.start()
+    own_col = pltpu.make_async_copy(ending, cols_ref.at[my_col], local_sem.at[1])
+
+    @pl.when(is_self)
+    def _():
+        own_col.start()
+
+    for o in range(1, 4):
+        at = pl.ds(pl.multiple_of(lax.rem(c + 4 - o, 4) * rows, rows), rows)
+        remote(ending, rows_ref.at[at], send.at[0], recv.at[7 + o], (s, r, c)).wait_recv()
+    for kk in range(2):
+        for zz in range(4):
+            i = kk * 4 + zz
+            local_one = jnp.logical_and(is_self, jnp.logical_and(kk == k, zz == c))
+
+            @pl.when(jnp.logical_not(local_one))
+            def _():
+                remote(ending, cols_ref.at[pl.ds(i * rows, rows)], send.at[0], recv.at[i], (s, r, c)).wait_recv()
+
+    own_row.wait()
+
+    @pl.when(is_self)
+    def _():
+        own_col.wait()
+
+    for cp in sends:
+        cp.wait_send()
+
+    @pl.when(jnp.logical_not(is_self))
+    def _():
+        self_cp.wait_send()
+
+
+def gathered(panel_index, piece, inverse, row_block, col_block):
+    rows = 2 * PANEL
+    vmem = pl.BlockSpec(memory_space=pltpu.VMEM)
+    return pl.pallas_call(
+        gather_kernel,
+        out_shape=(
+            jax.ShapeDtypeStruct((rows, PANEL), F32),
+            jax.ShapeDtypeStruct((row_block, PANEL), BF16),
+            jax.ShapeDtypeStruct((col_block, PANEL), BF16),
+        ),
+        in_specs=[pl.BlockSpec(memory_space=pltpu.SMEM), vmem, vmem],
+        out_specs=(vmem, vmem, vmem),
+        scratch_shapes=[
+            pltpu.VMEM((rows, PANEL), BF16),
+            pltpu.SemaphoreType.DMA((11,)),
+            pltpu.SemaphoreType.DMA((11,)),
+            pltpu.SemaphoreType.DMA((2,)),
+        ],
+        compiler_params=pltpu.CompilerParams(collective_id=1, has_side_effects=True),
+        name="factor_gather",
+    )(panel_index, piece, inverse)
+
+
+def direct(root_matrix, inverse_block, link_tiles, tile_mask, panel_index):
+    row_block, col_block = root_matrix.shape
+    tiles, diag = scenario_tiles(root_matrix, inverse_block[0], link_tiles[0], tile_mask, panel_index)
+    piece, diagonal = reduced(tiles, diag)
+    chol_lower = jnp.linalg.cholesky(diagonal)
+    inverse = jax.scipy.linalg.solve_triangular(chol_lower, jnp.eye(PANEL, dtype=F32), lower=True)
+    factor_rows, own_rows, own_cols = gathered(panel_index, piece, inverse, row_block, col_block)
+    update = lax.dot_general(
+        own_rows, own_cols, (((1,), (1,)), ((), ())), preferred_element_type=jnp.float32
+    )
+    return (root_matrix - update, factor_rows)
+
+
 def solution(mesh):
     in_specs = (
         P(("scen", "row"), "col"),
@@ -103,4 +470,6 @@
         P(),
     )
     out_specs = (P(("scen", "row"), "col"), P(("scen", "row", "col"), None))
-    return jax.shard_map(local, mesh=mesh, in_specs=in_specs, out_specs=out_specs, check_vma=False)
+    sizes = tuple(mesh.shape[a] for a in ("scen", "row", "col"))
+    body = direct if sizes == (2, 4, 4) else local
+    return jax.shard_map(body, mesh=mesh, in_specs=in_specs, out_specs=out_specs, check_vma=False)

time: 296 us -> 137 us (0.46)
  the two profiles are of different devices: /device:TPU:7 before, /device:TPU:0 now
where the time goes in v1:
time: 137 us
  Pallas kernels  97.6 us (71%)
  other arithmetic  22.9 us (17%)
  matrix products  9.21 us (7%)
  local copies, waits for them, and re-layouts  6.12 us (4%)
    pallas_call x1, Pallas kernels, reduced(): pl.pallas_call(sum_kernel, out_shape=(jax.ShapeDtypeStruct((2, *tile), F3...  46.5 us
    pallas_call x1, Pallas kernels, gathered(): pl.pallas_call(gather_kernel, out_shape=(jax.ShapeDtypeStruct((rows, PANE...  44.1 us
    another operation x3, other arithmetic, direct(): chol_lower = jnp.linalg.cholesky(diagonal)  12.4 us
    another operation x2, other arithmetic, direct(): jax.scipy.linalg.solve_triangular(chol_lower, jnp.eye(PANEL, dtype=F32),...  10.5 us
    dot_general x1, matrix products, direct(): lax.dot_general(own_rows, own_cols, (((1,), (1,)), ((), ())), preferred_e...  8.33 us
    pallas_call x1, Pallas kernels, scenario_tiles(): pl.pallas_call(term_kernel, out_shape=(jax.ShapeDtypeStruct((tile_total,...  6.93 us
    unnamed x11, local copies, waits for them, and re-layouts  6.03 us

profile of v1, /device:TPU:0, one launch (start us, length us, event | category | flops | bytes accessed | tf_op | source)
XLA Modules:
  0.0 137.1 jit_solution(9810211837675088167)
XLA Ops:
  1.3 0.0 copy-start
  1.3 2.5 %copy-done = bf16[1,20,1024,128]{3,2,1,0:T(8,128)(2,1)S(1)} copy-done((bf16[1,20,1024,128]{3,2,1,0:T(8,128)(2,1)S(1)}, bf16[1,20,1024,128]{3,2,1,0:T(8,128)(2,1)}, u32[]{:S(2)}) %copy-start) | copy-done | bytes 5242904
  3.8 0.0 copy-start.1
  3.8 1.6 %copy-done.1 = bf16[1,1024,1024]{2,1,0:T(8,128)(2,1)S(1)} copy-done((bf16[1,1024,1024]{2,1,0:T(8,128)(2,1)S(1)}, bf16[1,1024,1024]{2,1,0:T(8,128)(2,1)}, u32[]{:S(2)}) %copy-start.1) | copy-done | bytes 2097176
  5.4 0.0 copy-start.3
  5.4 0.7 copy-done.3
  6.0 6.9 %scenario_tiles.1 = (f32[64,128,128]{2,1,0:T(8,128)S(1)}, f32[128,128]{1,0:T(8,128)S(1)}) custom-call(s32[1]{0:T(128)S(6)} %copy.9.panel_ref, s32[1,64]{1,0:T(1,128)S(1)} %copy-done.3, bf16[1024,1024]{1,0:T(8,128)(2,1)S(1)} %bitcast.14, bf16[20,1024,128]{2,1,0:T(8,128)(2,1)S(1)} %bitcast.13, f32[1024,2048]{1,0:T(8,128)} %root_ref.1), custom_call_target="tpu_custom_call" | custom-call | tf_op jit(solution)/shard_map/scenario_tiles/pallas_call | solution.py:165
  12.9 46.5 %panel_sum.1 = (f32[2,128,128]{2,1,0:T(8,128)S(1)}, f32[128,128]{1,0:T(8,128)S(1)}) custom-call(f32[64,128,128]{2,1,0:T(8,128)S(1)} %get-tuple-element.9.tiles_hbm, f32[128,128]{1,0:T(8,128)S(1)} %get-tuple-element.10.diag_in), custom_call_target="tpu_custom_call" | custom-call | tf_op jit(solution)/shard_map/panel_sum/pallas_call | solution.py:311
  59.5 0.0 copy-start.2
  59.5 0.6 copy-done.2
  60.1 0.1 copy.7
  60.2 11.7 %cholesky.17 = f32[128,128]{1,0:T(8,128)S(1)} custom-call(f32[128,128]{1,0:T(8,128)S(1)} %fusion.3), custom_call_target="Cholesky" | custom-call | tf_op jit(solution)/shard_map/jit(cholesky)/cholesky | solution.py:455
  72.0 0.6 compare_reduce_fusion
  72.6 0.7 fusion
  73.3 9.8 %custom-call.7 = f32[1,128,128]{1,2,0:T(8,128)S(1)} custom-call(f32[1,128,128]{2,1,0:T(8,128)S(1)} %fusion), custom_call_target="InvertDiagBlocksLowerTriangular" | custom-call | tf_op jit(solution)/shard_map/jit(_solve_triangular)/triangular_solve | solution.py:456
  83.1 0.9 fusion.1.inv_ref
  84.0 44.1 %factor_gather.1 = (f32[256,128]{1,0:T(8,128)}, bf16[1024,128]{1,0:T(8,128)(2,1)}, bf16[2048,128]{1,0:T(8,128)(2,1)}) custom-call(s32[1]{0:T(128)S(6)} %copy.9.panel_ref, f32[2,128,128]{2,1,0:T(8,128)} %copy-done.2, f32[128,128]{1,0:T(8,128)} %fusion.1.inv_ref), custom_call_target="tpu_custom_call" | custom-call | tf_op jit(solution)/shard_map/factor_gather/pallas_call | solution.py:431
  128.1 0.0 copy-start.4
  128.1 8.3 %convolution_subtract_fusion = f32[1024,2048]{1,0:T(8,128)} fusion(f32[1024,2048]{1,0:T(8,128)} %root_ref.1, bf16[1024,128]{1,0:T(8,128)(2,1)} %get-tuple-element.13, bf16[2048,128]{1,0:T(8,128)(2,1)} %get-tuple-element.14), kind=kOutput, calls=%fused_computation | convolution fusion | flops 538968064 | bytes 17563648 | tf_op jit(solution)/shard_map/dot_general | solution.py:458
  136.5 0.0 copy-done.4
  136.5 0.7 copy.10
  (2 shorter events, 0.0 us)
Async XLA Ops:
  1.3 2.5 %copy-start = (bf16[1,20,1024,128]{3,2,1,0:T(8,128)(2,1)S(1)}, bf16[1,20,1024,128]{3,2,1,0:T(8,128)(2,1)}, u32[]{:S(2)}) copy-start(bf16[1,20,1024,128]{3,2,1,0:T(8,128)(2,1)} %param.7) | copy-start | bytes 15728644
  3.8 1.6 %copy-start.1 = (bf16[1,1024,1024]{2,1,0:T(8,128)(2,1)S(1)}, bf16[1,1024,1024]{2,1,0:T(8,128)(2,1)}, u32[]{:S(2)}) copy-start(bf16[1,1024,1024]{2,1,0:T(8,128)(2,1)} %param.6) | copy-start | bytes 6291460
  5.4 0.7 copy-start.3
  59.5 0.7 copy-start.2
  128.1 8.3 %copy-start.4 = (f32[256,128]{1,0:T(8,128)S(1)}, f32[256,128]{1,0:T(8,128)}, u32[]{:S(2)}) copy-start(f32[256,128]{1,0:T(8,128)} %get-tuple-element.19) | copy-start | bytes 393220

commit v2 on v1

--- a/solution.py
+++ b/solution.py
@@ -172,8 +172,8 @@
             num_scalar_prefetch=2,
             grid=(1,),
             in_specs=[
-                pl.BlockSpec(memory_space=pl.ANY),
-                pl.BlockSpec(memory_space=pl.ANY),
+                pl.BlockSpec(memory_space=pltpu.HBM),
+                pl.BlockSpec(memory_space=pltpu.HBM),
                 pl.BlockSpec((own_rows, PANEL), lambda i, p, m: (0, lax.rem(p[0], wide))),
             ],
             out_specs=[
@@ -187,7 +187,7 @@
                 pltpu.SemaphoreType.DMA((slots + 2,)),
             ],
         ),
-        compiler_params=pltpu.CompilerParams(vmem_limit_bytes=40 * 2**20),
+        compiler_params=pltpu.CompilerParams(vmem_limit_bytes=60 * 2**20),
         name="scenario_tiles",
     )(panel_index, tile_mask, inverse, tiles, root_matrix)
 
@@ -336,22 +336,28 @@
     )(tiles, diag)
 
 
-def gather_kernel(panel_ref, piece_ref, inv_ref, factor_ref, rows_ref, cols_ref, ending, send, recv, local_sem):
+def gather_kernel(panel_ref, piece_ref, inv_ref, factor_ref, rows_ref, cols_ref, send_z, recv_z,
+                  send_x, send_y, recv_p, send_c, recv_c):
     s, r, c = (lax.axis_index(a) for a in ("scen", "row", "col"))
     y, k = r // 2, lax.rem(r, 2)
     rows = factor_ref.shape[0]
-    to_col = 2 * s + y
-    is_self = to_col == c
+    far_x = lax.rem(s + c // 2, 2)
+    far_y = lax.rem(y + c, 2)
+    source = jnp.logical_and(far_x == 0, far_y == 0)
+    x_to = (1 - s, r, c)
+    y_to = (s, 2 * (1 - y) + k, c)
+    core = (s, 2 * y + 1 - k, c)
     barrier = pltpu.get_barrier_semaphore()
     for o in range(1, 4):
         pl.semaphore_signal(barrier, inc=1, device_id=(s, r, lax.rem(c + o, 4)), device_id_type=MESH_ID)
-    for kk in range(2):
-        for zz in range(4):
-            src = (c // 2, 2 * lax.rem(c, 2) + kk, zz)
-
-            @pl.when(jnp.logical_not(jnp.logical_and(is_self, jnp.logical_and(kk == k, zz == c))))
-            def _():
-                pl.semaphore_signal(barrier, inc=1, device_id=src, device_id_type=MESH_ID)
+    for dev in (x_to, y_to, core):
+        pl.semaphore_signal(barrier, inc=1, device_id=dev, device_id_type=MESH_ID)
+
+    def row_at(z):
+        return rows_ref.at[pl.ds(pl.multiple_of(z * rows, rows), rows)]
+
+    def col_at(kk, z):
+        return cols_ref.at[pl.ds(pl.multiple_of((kk * 4 + z) * rows, rows), rows)]
 
     f = panel_ref[0]
     first = (s * 4 + r) * (4 * rows) + c * rows
@@ -362,67 +368,67 @@
         )
         ids = first + i * PANEL + lax.broadcasted_iota(jnp.int32, part.shape, 0)
         factor_ref[i * PANEL : (i + 1) * PANEL, :] = jnp.where(ids >= f * PANEL, part, 0.0)
-        ending[i * PANEL : (i + 1) * PANEL, :] = jnp.where(ids >= f * PANEL + PANEL, part, 0.0).astype(BF16)
-
-    pl.semaphore_wait(barrier, jnp.where(is_self, 10, 11))
-
-    my_row = pl.ds(pl.multiple_of(c * rows, rows), rows)
-    my_slot = k * 4 + c
-    my_col = pl.ds(pl.multiple_of(my_slot * rows, rows), rows)
-    sends = []
-    n = 0
-    for ds_ in range(2):
-        for dr in range(4):
-            dev = (lax.rem(s + 1 - ds_, 2), lax.rem(r + 3 - dr, 4), to_col)
-            cp = remote(ending, cols_ref.at[my_col], send.at[n], recv.at[my_slot], dev)
-            n += 1
-            if ds_ == 1 and dr == 3:
-                self_cp = cp
-            else:
-                cp.start()
-                sends.append(cp)
-
-    @pl.when(jnp.logical_not(is_self))
+        ending = jnp.where(ids >= f * PANEL + PANEL, part, 0.0).astype(BF16)
+        rows_ref[pl.ds(pl.multiple_of(c * rows + i * PANEL, PANEL), PANEL), :] = ending
+
+    pl.semaphore_wait(barrier, 6)
+    z_copies = []
+    for o in range(1, 4):
+        cp = remote(row_at(c), row_at(c), send_z.at[o - 1], recv_z.at[o - 1], (s, r, lax.rem(c + o, 4)))
+        cp.start()
+        z_copies.append(cp)
+
+    def z_arrival(o):
+        remote(row_at(lax.rem(c + 4 - o, 4)), row_at(lax.rem(c + 4 - o, 4)), send_z.at[o - 1], recv_z.at[o - 1], core).wait_recv()
+
+    for o in range(4):
+        z = lax.rem(c + 4 - o, 4)
+        here = col_at(k, z)
+        to_x = remote(here, here, send_x.at[o], recv_p.at[o], x_to)
+        to_y = remote(here, here, send_y.at[o], recv_p.at[o], y_to)
+
+        @pl.when(source)
+        def _():
+            if o:
+                z_arrival(o)
+            here[...] = row_at(z)[...]
+            to_x.start()
+            to_y.start()
+
+        @pl.when(jnp.logical_not(source))
+        def _():
+            to_x.wait_recv()
+
+        @pl.when(jnp.logical_and(far_x == 1, far_y == 0) if o < 2 else jnp.logical_and(far_x == 0, far_y == 1))
+        def _():
+            (to_y if o < 2 else to_x).start()
+
+        remote(here, here, send_c.at[o], recv_c.at[o], core).start()
+
+    @pl.when(jnp.logical_not(source))
     def _():
-        self_cp.start()
-
-    for o in range(1, 4):
-        cp = remote(ending, rows_ref.at[my_row], send.at[n], recv.at[7 + o], (s, r, lax.rem(c + o, 4)))
-        cp.start()
-        n += 1
-        sends.append(cp)
-    own_row = pltpu.make_async_copy(ending, rows_ref.at[my_row], local_sem.at[0])
-    own_row.start()
-    own_col = pltpu.make_async_copy(ending, cols_ref.at[my_col], local_sem.at[1])
-
-    @pl.when(is_self)
-    def _():
-        own_col.start()
-
-    for o in range(1, 4):
-        at = pl.ds(pl.multiple_of(lax.rem(c + 4 - o, 4) * rows, rows), rows)
-        remote(ending, rows_ref.at[at], send.at[0], recv.at[7 + o], (s, r, c)).wait_recv()
-    for kk in range(2):
-        for zz in range(4):
-            i = kk * 4 + zz
-            local_one = jnp.logical_and(is_self, jnp.logical_and(kk == k, zz == c))
-
-            @pl.when(jnp.logical_not(local_one))
-            def _():
-                remote(ending, cols_ref.at[pl.ds(i * rows, rows)], send.at[0], recv.at[i], (s, r, c)).wait_recv()
-
-    own_row.wait()
-
-    @pl.when(is_self)
-    def _():
-        own_col.wait()
-
-    for cp in sends:
+        for o in range(1, 4):
+            z_arrival(o)
+
+    for o in range(4):
+        z = lax.rem(c + 4 - o, 4)
+        there, here = col_at(1 - k, z), col_at(k, z)
+        remote(there, there, send_c.at[o], recv_c.at[o], core).wait_recv()
+        remote(here, here, send_c.at[o], recv_c.at[o], core).wait_send()
+        to_x = remote(here, here, send_x.at[o], recv_p.at[o], x_to)
+        to_y = remote(here, here, send_y.at[o], recv_p.at[o], y_to)
+
+        @pl.when(source)
+        def _():
+            to_x.wait_send()
+            to_y.wait_send()
+
+        @pl.when(jnp.logical_and(far_x == 1, far_y == 0) if o < 2 else jnp.logical_and(far_x == 0, far_y == 1))
+        def _():
+            (to_y if o < 2 else to_x).wait_send()
+
+    for cp in z_copies:
         cp.wait_send()
-
-    @pl.when(jnp.logical_not(is_self))
-    def _():
-        self_cp.wait_send()
 
 
 def gathered(panel_index, piece, inverse, row_block, col_block):
@@ -438,10 +444,13 @@
         in_specs=[pl.BlockSpec(memory_space=pltpu.SMEM), vmem, vmem],
         out_specs=(vmem, vmem, vmem),
         scratch_shapes=[
-            pltpu.VMEM((rows, PANEL), BF16),
-            pltpu.SemaphoreType.DMA((11,)),
-            pltpu.SemaphoreType.DMA((11,)),
-            pltpu.SemaphoreType.DMA((2,)),
+            pltpu.SemaphoreType.DMA((3,)),
+            pltpu.SemaphoreType.DMA((3,)),
+            pltpu.SemaphoreType.DMA((4,)),
+            pltpu.SemaphoreType.DMA((4,)),
+            pltpu.SemaphoreType.DMA((4,)),
+            pltpu.SemaphoreType.DMA((4,)),
+            pltpu.SemaphoreType.DMA((4,)),
         ],
         compiler_params=pltpu.CompilerParams(collective_id=1, has_side_effects=True),
         name="factor_gather",

time: 137 us -> 111 us (0.81)
  the two profiles are of different devices: /device:TPU:0 before, /device:TPU:7 now
where the time goes in v2:
time: 111 us
  Pallas kernels  72.8 us (66%)
  other arithmetic  22.9 us (21%)
  matrix products  9.21 us (8%)
  local copies, waits for them, and re-layouts  4.42 us (4%)
  between operations  1.36 us (1%)
    pallas_call x1, Pallas kernels, reduced(): pl.pallas_call(sum_kernel, out_shape=(jax.ShapeDtypeStruct((2, *tile), F3...  42.8 us
    pallas_call x1, Pallas kernels, gathered(): pl.pallas_call(gather_kernel, out_shape=(jax.ShapeDtypeStruct((rows, PANE...  19.2 us
    another operation x3, other arithmetic, direct(): chol_lower = jnp.linalg.cholesky(diagonal)  12.4 us
    pallas_call x1, Pallas kernels, scenario_tiles(): pl.pallas_call(term_kernel, out_shape=(jax.ShapeDtypeStruct((tile_total,...  10.7 us
    another operation x2, other arithmetic, direct(): jax.scipy.linalg.solve_triangular(chol_lower, jnp.eye(PANEL, dtype=F32),...  10.5 us
    dot_general x1, matrix products, direct(): lax.dot_general(own_rows, own_cols, (((1,), (1,)), ((), ())), preferred_e...  8.33 us
    unnamed x9, local copies, waits for them, and re-layouts  4.33 us

profile of v2, /device:TPU:7, one launch (start us, length us, event | category | flops | bytes accessed | tf_op | source)
XLA Modules:
  0.0 110.6 jit_solution(10536881539291673761)
XLA Ops:
  1.3 10.7 %scenario_tiles.1 = (f32[64,128,128]{2,1,0:T(8,128)}, f32[128,128]{1,0:T(8,128)}) custom-call(s32[1]{0:T(128)S(6)} %copy.9.panel_ref, s32[1,64]{1,0:T(1,128)} %mask_ref.1, bf16[1024,1024]{1,0:T(8,128)(2,1)} %bitcast.14, bf16[20,1024,128]{2,1,0:T(8,128)(2,1)} %bitcast.13, f32[1024,2048]{1,0:T(8,128)} %root_ref.1), custom_call_target="tpu_custom_call" | custom-call | tf_op jit(solution)/shard_map/scenario_tiles/pallas_call | solution.py:165
  12.0 0.0 copy-start
  12.0 2.2 %copy-done = f32[64,128,128]{2,1,0:T(8,128)S(1)} copy-done((f32[64,128,128]{2,1,0:T(8,128)S(1)}, f32[64,128,128]{2,1,0:T(8,128)}, u32[]{:S(2)}) %copy-start) | copy-done | bytes 4194328
  14.2 0.0 copy-start.2
  14.2 0.8 copy-done.2
  15.1 42.8 %panel_sum.1 = (f32[2,128,128]{2,1,0:T(8,128)S(1)}, f32[128,128]{1,0:T(8,128)S(1)}) custom-call(f32[64,128,128]{2,1,0:T(8,128)S(1)} %copy-done, f32[128,128]{1,0:T(8,128)S(1)} %copy-done.2), custom_call_target="tpu_custom_call" | custom-call | tf_op jit(solution)/shard_map/panel_sum/pallas_call | solution.py:311
  57.9 0.0 copy-start.1
  57.9 0.6 copy-done.1
  58.6 0.1 copy.7
  58.7 11.7 %cholesky.17 = f32[128,128]{1,0:T(8,128)S(1)} custom-call(f32[128,128]{1,0:T(8,128)S(1)} %fusion.3), custom_call_target="Cholesky" | custom-call | tf_op jit(solution)/shard_map/jit(cholesky)/cholesky | solution.py:464
  70.4 0.6 compare_reduce_fusion
  71.1 0.7 fusion
  71.7 9.8 %custom-call.7 = f32[1,128,128]{1,2,0:T(8,128)S(1)} custom-call(f32[1,128,128]{2,1,0:T(8,128)S(1)} %fusion), custom_call_target="InvertDiagBlocksLowerTriangular" | custom-call | tf_op jit(solution)/shard_map/jit(_solve_triangular)/triangular_solve | solution.py:465
  81.5 0.9 fusion.1.inv_ref
  82.4 19.2 %factor_gather.1 = (f32[256,128]{1,0:T(8,128)}, bf16[1024,128]{1,0:T(8,128)(2,1)}, bf16[2048,128]{1,0:T(8,128)(2,1)}) custom-call(s32[1]{0:T(128)S(6)} %copy.9.panel_ref, f32[2,128,128]{2,1,0:T(8,128)} %copy-done.1, f32[128,128]{1,0:T(8,128)} %fusion.1.inv_ref), custom_call_target="tpu_custom_call" | custom-call | tf_op jit(solution)/shard_map/factor_gather/pallas_call | solution.py:437
  101.6 0.0 copy-start.3
  101.6 8.3 %convolution_subtract_fusion = f32[1024,2048]{1,0:T(8,128)} fusion(f32[1024,2048]{1,0:T(8,128)} %root_ref.1, bf16[1024,128]{1,0:T(8,128)(2,1)} %get-tuple-element.13, bf16[2048,128]{1,0:T(8,128)(2,1)} %get-tuple-element.14), kind=kOutput, calls=%fused_computation | convolution fusion | flops 538968064 | bytes 17563648 | tf_op jit(solution)/shard_map/dot_general | solution.py:467
  110.0 0.0 copy-done.3
  110.0 0.7 copy.10
  (2 shorter events, 0.0 us)
Async XLA Ops:
  12.0 2.2 %copy-start = (f32[64,128,128]{2,1,0:T(8,128)S(1)}, f32[64,128,128]{2,1,0:T(8,128)}, u32[]{:S(2)}) copy-start(f32[64,128,128]{2,1,0:T(8,128)} %get-tuple-element.9.tiles_hbm) | copy-start | bytes 12582916
  14.2 0.8 copy-start.2
  57.9 0.7 copy-start.1
  101.6 8.3 %copy-start.3 = (f32[256,128]{1,0:T(8,128)S(1)}, f32[256,128]{1,0:T(8,128)}, u32[]{:S(2)}) copy-start(f32[256,128]{1,0:T(8,128)} %get-tuple-element.19) | copy-start | bytes 393220

commit v3 on v2

--- a/solution.py
+++ b/solution.py
@@ -198,8 +198,123 @@
     )
 
 
-def sum_kernel(tiles_hbm, diag_in, piece_ref, diag_ref, own, got0, got1, got2, acc, got3, got4,
-               dsum, dgot, dpart, dparts, send, recv, local_sem, dsend, drecv):
+def invert_blocks(state, inv_ref, start, stop):
+    lane = lax.broadcasted_iota(jnp.int32, (8, PANEL), 1)
+    sub = lax.broadcasted_iota(jnp.int32, (8, 1), 0)
+
+    def block(b, carry):
+        at = pl.ds(pl.multiple_of(b * 8, 8), 8)
+        strip = state[at, :]
+        for i in range(8):
+            col = jnp.sum(jnp.where(lane == b * 8 + i, strip[:, :PANEL], 0.0), axis=1, keepdims=True)
+            pivot = col[i : i + 1, :]
+            inv = lax.rsqrt(pivot)
+            inv = inv * (1.5 - 0.5 * pivot * inv * inv)
+            row = strip[i : i + 1, :] * inv
+            coef = jnp.where(sub > i, col * inv, 0.0)
+            strip = jnp.where(sub == i, row, strip - coef * row)
+        inv_ref[at, :] = strip[:, PANEL:]
+        later = jnp.where(lane >= b * 8 + 8, strip[:, :PANEL], 0.0)
+        state[...] = state[...] - lax.dot_general(
+            later, strip, (((0,), (0,)), ((), ())), preferred_element_type=F32, precision=lax.Precision.HIGHEST
+        )
+        return carry
+
+    lax.fori_loop(start, stop, block, 0)
+
+
+def gather_phase(panel_ref, piece_ref, inv_ref, factor_ref, rows_ref, cols_ref, send_z, recv_z,
+                 send_x, send_y, recv_p, send_c, recv_c):
+    s, r, c = (lax.axis_index(a) for a in ("scen", "row", "col"))
+    y, k = r // 2, lax.rem(r, 2)
+    rows = factor_ref.shape[0]
+    far_x = lax.rem(s + c // 2, 2)
+    far_y = lax.rem(y + c, 2)
+    source = jnp.logical_and(far_x == 0, far_y == 0)
+    x_to = (1 - s, r, c)
+    y_to = (s, 2 * (1 - y) + k, c)
+    core = (s, 2 * y + 1 - k, c)
+
+    def row_at(z):
+        return rows_ref.at[pl.ds(pl.multiple_of(z * rows, rows), rows)]
+
+    def col_at(kk, z):
+        return cols_ref.at[pl.ds(pl.multiple_of((kk * 4 + z) * rows, rows), rows)]
+
+    f = panel_ref[0]
+    first = (s * 4 + r) * (4 * rows) + c * rows
+    for i in range(2):
+        part = lax.dot_general(
+            piece_ref[i], inv_ref[...], (((0,), (1,)), ((), ())),
+            preferred_element_type=F32, precision=lax.Precision.HIGHEST,
+        )
+        ids = first + i * PANEL + lax.broadcasted_iota(jnp.int32, part.shape, 0)
+        factor_ref[i * PANEL : (i + 1) * PANEL, :] = jnp.where(ids >= f * PANEL, part, 0.0)
+        ending = jnp.where(ids >= f * PANEL + PANEL, part, 0.0).astype(BF16)
+        rows_ref[pl.ds(pl.multiple_of(c * rows + i * PANEL, PANEL), PANEL), :] = ending
+
+    z_copies = []
+    for o in range(1, 4):
+        cp = remote(row_at(c), row_at(c), send_z.at[o - 1], recv_z.at[o - 1], (s, r, lax.rem(c + o, 4)))
+        cp.start()
+        z_copies.append(cp)
+
+    def z_arrival(o):
+        remote(row_at(lax.rem(c + 4 - o, 4)), row_at(lax.rem(c + 4 - o, 4)), send_z.at[o - 1], recv_z.at[o - 1], core).wait_recv()
+
+    for o in range(4):
+        z = lax.rem(c + 4 - o, 4)
+        here = col_at(k, z)
+        to_x = remote(here, here, send_x.at[o], recv_p.at[o], x_to)
+        to_y = remote(here, here, send_y.at[o], recv_p.at[o], y_to)
+
+        @pl.when(source)
+        def _():
+            if o:
+                z_arrival(o)
+            here[...] = row_at(z)[...]
+            to_x.start()
+            to_y.start()
+
+        @pl.when(jnp.logical_not(source))
+        def _():
+            to_x.wait_recv()
+
+        @pl.when(jnp.logical_and(far_x == 1, far_y == 0) if o < 2 else jnp.logical_and(far_x == 0, far_y == 1))
+        def _():
+            (to_y if o < 2 else to_x).start()
+
+        remote(here, here, send_c.at[o], recv_c.at[o], core).start()
+
+    @pl.when(jnp.logical_not(source))
+    def _():
+        for o in range(1, 4):
+            z_arrival(o)
+
+    for o in range(4):
+        z = lax.rem(c + 4 - o, 4)
+        there, here = col_at(1 - k, z), col_at(k, z)
+        remote(there, there, send_c.at[o], recv_c.at[o], core).wait_recv()
+        remote(here, here, send_c.at[o], recv_c.at[o], core).wait_send()
+        to_x = remote(here, here, send_x.at[o], recv_p.at[o], x_to)
+        to_y = remote(here, here, send_y.at[o], recv_p.at[o], y_to)
+
+        @pl.when(source)
+        def _():
+            to_x.wait_send()
+            to_y.wait_send()
+
+        @pl.when(jnp.logical_and(far_x == 1, far_y == 0) if o < 2 else jnp.logical_and(far_x == 0, far_y == 1))
+        def _():
+            (to_y if o < 2 else to_x).wait_send()
+
+    for cp in z_copies:
+        cp.wait_send()
+
+
+def panel_kernel(panel_ref, tiles_hbm, diag_in, factor_ref, rows_ref, cols_ref, own, got0, got1, got2, acc, got3, got4,
+                 dsum, dgot, dpart, dparts, diag_ref, state, inv_ref, piece_ref, send, recv, local_sem, dsend, drecv,
+                 *gather_sems):
     s, r, c = (lax.axis_index(a) for a in ("scen", "row", "col"))
     y, k = r // 2, lax.rem(r, 2)
     core = (s, 2 * y + 1 - k, c)
@@ -267,6 +382,14 @@
         cp = remote(dpart, diag_ref.at[pl.ds(pl.multiple_of(me * 8, 8), 8)], dsend.at[15 + o], drecv.at[15 + o], dev)
         cp.start()
         out2.append(cp)
+    for cp in out2:
+        cp.wait_recv()
+    full = diag_ref[...]
+    state[:, :PANEL] = 0.5 * (full + full.T)
+    state[:, PANEL:] = jnp.where(
+        lax.broadcasted_iota(jnp.int32, (PANEL, PANEL), 0) == lax.broadcasted_iota(jnp.int32, (PANEL, PANEL), 1), 1.0, 0.0
+    )
+    invert_blocks(state, inv_ref, 0, 3)
     ax[0][0].wait_recv()
     acc[0, 0] = own[s * 2 + 1 - y, 0:4] + got1[0, 0]
     a2 = remote(acc.at[0, 0], got2.at[0], send.at[8], recv.at[8], y_to)
@@ -275,6 +398,7 @@
     acc[0, 1] = own[(1 - s) * 2 + y, 4:8] + got1[1, 0]
     b2 = remote(acc.at[0, 1], got2.at[1], send.at[9], recv.at[9], x_to)
     b2.start()
+    invert_blocks(state, inv_ref, 3, 9)
     ax[1][0].wait_recv()
     acc[1, 0] = own[s * 2 + y, 0:4] + got1[0, 1]
     ax[1][1].wait_recv()
@@ -290,6 +414,7 @@
         cp = remote(acc.at[1, h, pl.ds((1 - par) * 2, 2)], got3.at[h], send.at[10 + h], recv.at[10 + h], (s, r, z1))
         cp.start()
         z_out.append(cp)
+    invert_blocks(state, inv_ref, 9, 13)
     z_out[0].wait_recv()
     z_out[1].wait_recv()
     a2.wait_send()
@@ -297,22 +422,26 @@
     last = remote(acc.at[0, 0, pl.ds(0, 2)], got4, send.at[12], recv.at[12], (s, r, z2))
     last.start()
     mine = acc[1, hi, pl.ds(par * 2, 2)] + got3[hi]
+    invert_blocks(state, inv_ref, 13, 16)
     last.wait_recv()
     piece_ref[...] = mine + got4[...]
-    for cp in out2:
-        cp.wait_recv()
+    gather_phase(panel_ref, piece_ref, inv_ref, factor_ref, rows_ref, cols_ref, *gather_sems)
     for cp in out1 + out2 + [ax[0][0], ax[0][1], ax[1][0], ax[1][1], b2, *z_out, last]:
         cp.wait_send()
 
 
-def reduced(tiles, diag):
+def panel_factor(panel_index, tiles, diag, row_block, col_block):
     tile = tiles.shape[1:]
     vmem = pl.BlockSpec(memory_space=pltpu.VMEM)
     return pl.pallas_call(
-        sum_kernel,
-        out_shape=(jax.ShapeDtypeStruct((2, *tile), F32), jax.ShapeDtypeStruct((PANEL, PANEL), F32)),
-        in_specs=[pl.BlockSpec(memory_space=pl.ANY), vmem],
-        out_specs=(vmem, vmem),
+        panel_kernel,
+        out_shape=(
+            jax.ShapeDtypeStruct((2 * PANEL, PANEL), F32),
+            jax.ShapeDtypeStruct((row_block, PANEL), BF16),
+            jax.ShapeDtypeStruct((col_block, PANEL), BF16),
+        ),
+        in_specs=[pl.BlockSpec(memory_space=pltpu.SMEM), pl.BlockSpec(memory_space=pl.ANY), vmem],
+        out_specs=(vmem, vmem, vmem),
         scratch_shapes=[
             pltpu.VMEM((4, 8, *tile), F32),
             pltpu.VMEM((4, 8, *tile), F32),
@@ -325,145 +454,28 @@
             pltpu.VMEM(tile, F32),
             pltpu.VMEM((8, PANEL), F32),
             pltpu.VMEM((16, 8, PANEL), F32),
+            pltpu.VMEM(tile, F32),
+            pltpu.VMEM((PANEL, 2 * PANEL), F32),
+            pltpu.VMEM(tile, F32),
+            pltpu.VMEM((2, *tile), F32),
             pltpu.SemaphoreType.DMA((13,)),
             pltpu.SemaphoreType.DMA((13,)),
             pltpu.SemaphoreType.DMA((4,)),
             pltpu.SemaphoreType.DMA((31,)),
             pltpu.SemaphoreType.DMA((31,)),
-        ],
-        compiler_params=pltpu.CompilerParams(collective_id=0, has_side_effects=True, vmem_limit_bytes=32 * 2**20),
-        name="panel_sum",
-    )(tiles, diag)
-
-
-def gather_kernel(panel_ref, piece_ref, inv_ref, factor_ref, rows_ref, cols_ref, send_z, recv_z,
-                  send_x, send_y, recv_p, send_c, recv_c):
-    s, r, c = (lax.axis_index(a) for a in ("scen", "row", "col"))
-    y, k = r // 2, lax.rem(r, 2)
-    rows = factor_ref.shape[0]
-    far_x = lax.rem(s + c // 2, 2)
-    far_y = lax.rem(y + c, 2)
-    source = jnp.logical_and(far_x == 0, far_y == 0)
-    x_to = (1 - s, r, c)
-    y_to = (s, 2 * (1 - y) + k, c)
-    core = (s, 2 * y + 1 - k, c)
-    barrier = pltpu.get_barrier_semaphore()
-    for o in range(1, 4):
-        pl.semaphore_signal(barrier, inc=1, device_id=(s, r, lax.rem(c + o, 4)), device_id_type=MESH_ID)
-    for dev in (x_to, y_to, core):
-        pl.semaphore_signal(barrier, inc=1, device_id=dev, device_id_type=MESH_ID)
-
-    def row_at(z):
-        return rows_ref.at[pl.ds(pl.multiple_of(z * rows, rows), rows)]
-
-    def col_at(kk, z):
-        return cols_ref.at[pl.ds(pl.multiple_of((kk * 4 + z) * rows, rows), rows)]
-
-    f = panel_ref[0]
-    first = (s * 4 + r) * (4 * rows) + c * rows
-    for i in range(2):
-        part = lax.dot_general(
-            piece_ref[i], inv_ref[...], (((0,), (1,)), ((), ())),
-            preferred_element_type=F32, precision=lax.Precision.HIGHEST,
-        )
-        ids = first + i * PANEL + lax.broadcasted_iota(jnp.int32, part.shape, 0)
-        factor_ref[i * PANEL : (i + 1) * PANEL, :] = jnp.where(ids >= f * PANEL, part, 0.0)
-        ending = jnp.where(ids >= f * PANEL + PANEL, part, 0.0).astype(BF16)
-        rows_ref[pl.ds(pl.multiple_of(c * rows + i * PANEL, PANEL), PANEL), :] = ending
-
-    pl.semaphore_wait(barrier, 6)
-    z_copies = []
-    for o in range(1, 4):
-        cp = remote(row_at(c), row_at(c), send_z.at[o - 1], recv_z.at[o - 1], (s, r, lax.rem(c + o, 4)))
-        cp.start()
-        z_copies.append(cp)
-
-    def z_arrival(o):
-        remote(row_at(lax.rem(c + 4 - o, 4)), row_at(lax.rem(c + 4 - o, 4)), send_z.at[o - 1], recv_z.at[o - 1], core).wait_recv()
-
-    for o in range(4):
-        z = lax.rem(c + 4 - o, 4)
-        here = col_at(k, z)
-        to_x = remote(here, here, send_x.at[o], recv_p.at[o], x_to)
-        to_y = remote(here, here, send_y.at[o], recv_p.at[o], y_to)
-
-        @pl.when(source)
-        def _():
-            if o:
-                z_arrival(o)
-            here[...] = row_at(z)[...]
-            to_x.start()
-            to_y.start()
-
-        @pl.when(jnp.logical_not(source))
-        def _():
-            to_x.wait_recv()
-
-        @pl.when(jnp.logical_and(far_x == 1, far_y == 0) if o < 2 else jnp.logical_and(far_x == 0, far_y == 1))
-        def _():
-            (to_y if o < 2 else to_x).start()
-
-        remote(here, here, send_c.at[o], recv_c.at[o], core).start()
-
-    @pl.when(jnp.logical_not(source))
-    def _():
-        for o in range(1, 4):
-            z_arrival(o)
-
-    for o in range(4):
-        z = lax.rem(c + 4 - o, 4)
-        there, here = col_at(1 - k, z), col_at(k, z)
-        remote(there, there, send_c.at[o], recv_c.at[o], core).wait_recv()
-        remote(here, here, send_c.at[o], recv_c.at[o], core).wait_send()
-        to_x = remote(here, here, send_x.at[o], recv_p.at[o], x_to)
-        to_y = remote(here, here, send_y.at[o], recv_p.at[o], y_to)
-
-        @pl.when(source)
-        def _():
-            to_x.wait_send()
-            to_y.wait_send()
-
-        @pl.when(jnp.logical_and(far_x == 1, far_y == 0) if o < 2 else jnp.logical_and(far_x == 0, far_y == 1))
-        def _():
-            (to_y if o < 2 else to_x).wait_send()
-
-    for cp in z_copies:
-        cp.wait_send()
-
-
-def gathered(panel_index, piece, inverse, row_block, col_block):
-    rows = 2 * PANEL
-    vmem = pl.BlockSpec(memory_space=pltpu.VMEM)
-    return pl.pallas_call(
-        gather_kernel,
-        out_shape=(
-            jax.ShapeDtypeStruct((rows, PANEL), F32),
-            jax.ShapeDtypeStruct((row_block, PANEL), BF16),
-            jax.ShapeDtypeStruct((col_block, PANEL), BF16),
-        ),
-        in_specs=[pl.BlockSpec(memory_space=pltpu.SMEM), vmem, vmem],
-        out_specs=(vmem, vmem, vmem),
-        scratch_shapes=[
             pltpu.SemaphoreType.DMA((3,)),
             pltpu.SemaphoreType.DMA((3,)),
-            pltpu.SemaphoreType.DMA((4,)),
-            pltpu.SemaphoreType.DMA((4,)),
-            pltpu.SemaphoreType.DMA((4,)),
-            pltpu.SemaphoreType.DMA((4,)),
-            pltpu.SemaphoreType.DMA((4,)),
+            *[pltpu.SemaphoreType.DMA((4,))] * 5,
         ],
-        compiler_params=pltpu.CompilerParams(collective_id=1, has_side_effects=True),
-        name="factor_gather",
-    )(panel_index, piece, inverse)
+        compiler_params=pltpu.CompilerParams(collective_id=0, has_side_effects=True, vmem_limit_bytes=60 * 2**20),
+        name="panel_factor",
+    )(panel_index, tiles, diag)
 
 
 def direct(root_matrix, inverse_block, link_tiles, tile_mask, panel_index):
     row_block, col_block = root_matrix.shape
     tiles, diag = scenario_tiles(root_matrix, inverse_block[0], link_tiles[0], tile_mask, panel_index)
-    piece, diagonal = reduced(tiles, diag)
-    chol_lower = jnp.linalg.cholesky(diagonal)
-    inverse = jax.scipy.linalg.solve_triangular(chol_lower, jnp.eye(PANEL, dtype=F32), lower=True)
-    factor_rows, own_rows, own_cols = gathered(panel_index, piece, inverse, row_block, col_block)
+    factor_rows, own_rows, own_cols = panel_factor(panel_index, tiles, diag, row_block, col_block)
     update = lax.dot_general(
         own_rows, own_cols, (((1,), (1,)), ((), ())), preferred_element_type=jnp.float32
     )

time: 111 us -> 86.3 us (0.78)
  other arithmetic: 22.9 us -> 0 us
  local copies, waits for them, and re-layouts: 4.42 us -> 0.66 us
  Pallas kernels: 72.8 us -> 76.1 us
    another operation x5 -> x0, other arithmetic: 22.9 us -> none  [the longest x3 12.4 us: direct(): chol_lower = jnp.linalg.cholesky(diagonal)]
    unnamed x9 -> x3, local copies, waits for them, and re-layouts: 4.33 us -> 0.66 us
    pallas_call x2 -> x1, Pallas kernels: 62 us -> 65.6 us  [panel_factor(): pl.pallas_call(panel_kernel, out_shape=(jax.ShapeDtypeStruct((2 * PANEL,...]
where the time goes in v3:
time: 86.3 us; the launch traced here: 86.4 us
  Pallas kernels  76.1 us (88%)
  matrix products  8.33 us (10%)
  between operations  1.3 us (2%)
    pallas_call x1, Pallas kernels, panel_factor(): pl.pallas_call(panel_kernel, out_shape=(jax.ShapeDtypeStruct((2 * PANEL,...  65.6 us
    pallas_call x1, Pallas kernels, scenario_tiles(): pl.pallas_call(term_kernel, out_shape=(jax.ShapeDtypeStruct((tile_total,...  10.5 us
    dot_general x1, matrix products, direct(): lax.dot_general(own_rows, own_cols, (((1,), (1,)), ((), ())), preferred_e...  8.33 us

profile of v3, /device:TPU:7, one launch (start us, length us, event | category | flops | bytes accessed | tf_op | source)
XLA Modules:
  0.0 86.4 jit_solution(9855814289726523795)
XLA Ops:
  1.3 10.5 %scenario_tiles.1 = (f32[64,128,128]{2,1,0:T(8,128)}, f32[128,128]{1,0:T(8,128)}) custom-call(s32[1]{0:T(128)S(6)} %copy.8.panel_ref, s32[1,64]{1,0:T(1,128)} %mask_ref.1, bf16[1024,1024]{1,0:T(8,128)(2,1)} %bitcast.5, bf16[20,1024,128]{2,1,0:T(8,128)(2,1)} %bitcast.4, f32[1024,2048]{1,0:T(8,128)} %root_ref.1), custom_call_target="tpu_custom_call" | custom-call | tf_op jit(solution)/shard_map/scenario_tiles/pallas_call | solution.py:165
  11.8 65.6 %panel_factor.1 = (f32[256,128]{1,0:T(8,128)}, bf16[1024,128]{1,0:T(8,128)(2,1)}, bf16[2048,128]{1,0:T(8,128)(2,1)}) custom-call(s32[1]{0:T(128)S(6)} %copy.8.panel_ref, f32[64,128,128]{2,1,0:T(8,128)} %get-tuple-element.7.tiles_hbm, f32[128,128]{1,0:T(8,128)} %get-tuple-element.8.diag_in), custom_call_target="tpu_custom_call" | custom-call | tf_op jit(solution)/shard_map/panel_factor/pallas_call | solution.py:436
  77.4 0.0 copy-start
  77.4 8.3 %convolution_subtract_fusion = f32[1024,2048]{1,0:T(8,128)} fusion(f32[1024,2048]{1,0:T(8,128)} %root_ref.1, bf16[1024,128]{1,0:T(8,128)(2,1)} %get-tuple-element.9, bf16[2048,128]{1,0:T(8,128)(2,1)} %get-tuple-element.10), kind=kOutput, calls=%fused_computation | convolution fusion | flops 538968064 | bytes 17563648 | tf_op jit(solution)/shard_map/dot_general | solution.py:479
  85.7 0.0 copy-done
  85.7 0.7 copy.9
Async XLA Ops:
  77.4 8.3 %copy-start = (f32[256,128]{1,0:T(8,128)S(1)}, f32[256,128]{1,0:T(8,128)}, u32[]{:S(2)}) copy-start(f32[256,128]{1,0:T(8,128)} %get-tuple-element.15) | copy-start | bytes 393220

commit v4 on v3

--- a/solution.py
+++ b/solution.py
@@ -312,7 +312,7 @@
         cp.wait_send()
 
 
-def panel_kernel(panel_ref, tiles_hbm, diag_in, factor_ref, rows_ref, cols_ref, own, got0, got1, got2, acc, got3, got4,
+def panel_kernel(panel_ref, tiles_hbm, diag_in, factor_ref, rows_ref, cols_ref, own, got0, got1, got2, onward, acc, got3, got4, final,
                  dsum, dgot, dpart, dparts, diag_ref, state, inv_ref, piece_ref, send, recv, local_sem, dsend, drecv,
                  *gather_sems):
     s, r, c = (lax.axis_index(a) for a in ("scen", "row", "col"))
@@ -336,17 +336,24 @@
 
     core_diag = remote(diag_in, dgot, dsend.at[0], drecv.at[0], core)
     core_diag.start()
+    far = (1 - s) * 2 + 1 - y
+    over_x = (1 - s) * 2 + y
+    over_y = s * 2 + 1 - y
+    here = s * 2 + y
+    par = lax.rem(c, 2)
+    hi = c // 2
+    order = (far, over_x, over_y, here)
     core_copy = []
     loads = []
-    for sp in range(2):
-        for yp in range(2):
-            i = sp * 2 + yp
-            cp = remote(tiles_hbm.at[pl.ds((i * 2 + 1 - k) * 8, 8)], got0.at[i], send.at[i], recv.at[i], core)
-            cp.start()
-            core_copy.append(cp)
-            ld = pltpu.make_async_copy(tiles_hbm.at[pl.ds((i * 2 + k) * 8, 8)], own.at[i], local_sem.at[i])
-            ld.start()
-            loads.append(ld)
+    for n, i in enumerate(order):
+        theirs = pl.ds(pl.multiple_of((i * 2 + 1 - k) * 8, 8), 8)
+        ours = pl.ds(pl.multiple_of((i * 2 + k) * 8, 8), 8)
+        cp = remote(tiles_hbm.at[theirs], got0.at[n], send.at[n], recv.at[n], core)
+        cp.start()
+        core_copy.append(cp)
+        ld = pltpu.make_async_copy(tiles_hbm.at[ours], own.at[n], local_sem.at[n])
+        ld.start()
+        loads.append(ld)
     core_diag.wait()
     dsum[...] = diag_in[...] + dgot[...]
     out1 = []
@@ -355,20 +362,29 @@
         cp = remote(dsum.at[pl.ds(pl.multiple_of(q * 8, 8), 8)], dparts.at[o], dsend.at[o], drecv.at[o], dev)
         cp.start()
         out1.append(cp)
-    for i in range(4):
-        loads[i].wait()
-        core_copy[i].wait()
-        own[i] = own[i] + got0[i]
-    order = []
-    ax = []
-    for step in range(2):
-        yy = (1 - y) if step == 0 else y
-        ss = (1 - s) if step == 0 else s
-        a = remote(own.at[(1 - s) * 2 + yy, pl.ds(0, 4)], got1.at[0, step], send.at[4 + step], recv.at[4 + step], x_to)
-        b = remote(own.at[ss * 2 + 1 - y, pl.ds(4, 4)], got1.at[1, step], send.at[6 + step], recv.at[6 + step], y_to)
-        a.start()
-        b.start()
-        ax.append((a, b))
+
+    pair = (2 * (1 - par), 2 * par)
+
+    def crossing(j, h, step):
+        n = 0 if step == 0 else 1 + h
+        at = 4 + (j * 2 + h) * 2 + step
+        return remote(own.at[n, pl.ds(4 * h + pair[j], 2)], got1.at[h, j, step], send.at[at], recv.at[at], y_to if h else x_to)
+
+    first = [[[crossing(j, h, step) for step in range(2)] for h in range(2)] for j in range(2)]
+
+    def pair_sum(n):
+        loads[n].wait()
+        core_copy[n].wait_recv()
+        own[n] = own[n] + got0[n]
+
+    pair_sum(0)
+    first[0][0][0].start()
+    first[0][1][0].start()
+    pair_sum(1)
+    first[0][0][1].start()
+    pair_sum(2)
+    first[0][1][1].start()
+    pair_sum(3)
     for cp in out1:
         cp.wait_recv()
     total = dsum[pl.ds(pl.multiple_of(me * 8, 8), 8), :]
@@ -382,52 +398,55 @@
         cp = remote(dpart, diag_ref.at[pl.ds(pl.multiple_of(me * 8, 8), 8)], dsend.at[15 + o], drecv.at[15 + o], dev)
         cp.start()
         out2.append(cp)
-    for cp in out2:
-        cp.wait_recv()
-    full = diag_ref[...]
-    state[:, :PANEL] = 0.5 * (full + full.T)
-    state[:, PANEL:] = jnp.where(
-        lax.broadcasted_iota(jnp.int32, (PANEL, PANEL), 0) == lax.broadcasted_iota(jnp.int32, (PANEL, PANEL), 1), 1.0, 0.0
-    )
-    invert_blocks(state, inv_ref, 0, 3)
-    ax[0][0].wait_recv()
-    acc[0, 0] = own[s * 2 + 1 - y, 0:4] + got1[0, 0]
-    a2 = remote(acc.at[0, 0], got2.at[0], send.at[8], recv.at[8], y_to)
-    a2.start()
-    ax[0][1].wait_recv()
-    acc[0, 1] = own[(1 - s) * 2 + y, 4:8] + got1[1, 0]
-    b2 = remote(acc.at[0, 1], got2.at[1], send.at[9], recv.at[9], x_to)
-    b2.start()
-    invert_blocks(state, inv_ref, 3, 9)
-    ax[1][0].wait_recv()
-    acc[1, 0] = own[s * 2 + y, 0:4] + got1[0, 1]
-    ax[1][1].wait_recv()
-    acc[1, 1] = own[s * 2 + y, 4:8] + got1[1, 1]
-    a2.wait_recv()
-    acc[1, 0] = acc[1, 0] + got2[0]
-    b2.wait_recv()
-    acc[1, 1] = acc[1, 1] + got2[1]
-    par = lax.rem(c, 2)
-    hi = c // 2
-    z_out = []
-    for h in range(2):
-        cp = remote(acc.at[1, h, pl.ds((1 - par) * 2, 2)], got3.at[h], send.at[10 + h], recv.at[10 + h], (s, r, z1))
-        cp.start()
-        z_out.append(cp)
-    invert_blocks(state, inv_ref, 9, 13)
-    z_out[0].wait_recv()
-    z_out[1].wait_recv()
-    a2.wait_send()
-    acc[0, 0, pl.ds(0, 2)] = acc[1, 1 - hi, pl.ds(par * 2, 2)] + got3[1 - hi]
-    last = remote(acc.at[0, 0, pl.ds(0, 2)], got4, send.at[12], recv.at[12], (s, r, z2))
+    second = []
+    for j in range(2):
+        for h in range(2):
+            first[j][h][0].wait_recv()
+            onward[j, h] = own[2 - h, pl.ds(4 * h + pair[j], 2)] + got1[h, j, 0]
+            at = 12 + j * 2 + h
+            cp = remote(onward.at[j, h], got2.at[j, h], send.at[at], recv.at[at], x_to if h else y_to)
+            cp.start()
+            second.append(cp)
+            if j == 0:
+                first[1][h][0].start()
+        if j == 0:
+            for cp in out2:
+                cp.wait_recv()
+            full = diag_ref[...]
+            state[:, :PANEL] = 0.5 * (full + full.T)
+            state[:, PANEL:] = jnp.where(
+                lax.broadcasted_iota(jnp.int32, (PANEL, PANEL), 0) == lax.broadcasted_iota(jnp.int32, (PANEL, PANEL), 1),
+                1.0, 0.0,
+            )
+        invert_blocks(state, inv_ref, (0, 6)[j], (2, 9)[j])
+        for h in range(2):
+            first[j][h][1].wait_recv()
+            acc[j, h] = own[3, pl.ds(4 * h + pair[j], 2)] + got1[h, j, 1]
+            if j == 0:
+                first[1][h][1].start()
+        invert_blocks(state, inv_ref, (2, 9)[j], (4, 12)[j])
+        for h in range(2):
+            second[2 * j + h].wait_recv()
+            acc[j, h] = acc[j, h] + got2[j, h]
+        if j == 0:
+            z_out = remote(acc.at[0], got3, send.at[16], recv.at[16], (s, r, z1))
+            z_out.start()
+            invert_blocks(state, inv_ref, 4, 6)
+    z_out.wait_recv()
+    final[...] = acc[1, 1 - hi] + got3[1 - hi]
+    last = remote(final, got4, send.at[17], recv.at[17], (s, r, z2))
     last.start()
-    mine = acc[1, hi, pl.ds(par * 2, 2)] + got3[hi]
-    invert_blocks(state, inv_ref, 13, 16)
+    mine = acc[1, hi] + got3[hi]
+    invert_blocks(state, inv_ref, 12, 16)
     last.wait_recv()
     piece_ref[...] = mine + got4[...]
+    for cp in core_copy + out1 + out2 + second + [z_out, last]:
+        cp.wait_send()
+    for j in range(2):
+        for h in range(2):
+            for step in range(2):
+                first[j][h][step].wait_send()
     gather_phase(panel_ref, piece_ref, inv_ref, factor_ref, rows_ref, cols_ref, *gather_sems)
-    for cp in out1 + out2 + [ax[0][0], ax[0][1], ax[1][0], ax[1][1], b2, *z_out, last]:
-        cp.wait_send()
 
 
 def panel_factor(panel_index, tiles, diag, row_block, col_block):
@@ -445,10 +464,12 @@
         scratch_shapes=[
             pltpu.VMEM((4, 8, *tile), F32),
             pltpu.VMEM((4, 8, *tile), F32),
-            pltpu.VMEM((2, 2, 4, *tile), F32),
-            pltpu.VMEM((2, 4, *tile), F32),
-            pltpu.VMEM((2, 2, 4, *tile), F32),
+            pltpu.VMEM((2, 2, 2, 2, *tile), F32),
+            pltpu.VMEM((2, 2, 2, *tile), F32),
+            pltpu.VMEM((2, 2, 2, *tile), F32),
+            pltpu.VMEM((2, 2, 2, *tile), F32),
             pltpu.VMEM((2, 2, *tile), F32),
+            pltpu.VMEM((2, *tile), F32),
             pltpu.VMEM((2, *tile), F32),
             pltpu.VMEM(tile, F32),
             pltpu.VMEM(tile, F32),
@@ -458,8 +479,8 @@
             pltpu.VMEM((PANEL, 2 * PANEL), F32),
             pltpu.VMEM(tile, F32),
             pltpu.VMEM((2, *tile), F32),
-            pltpu.SemaphoreType.DMA((13,)),
-            pltpu.SemaphoreType.DMA((13,)),
+            pltpu.SemaphoreType.DMA((18,)),
+            pltpu.SemaphoreType.DMA((18,)),
             pltpu.SemaphoreType.DMA((4,)),
             pltpu.SemaphoreType.DMA((31,)),
             pltpu.SemaphoreType.DMA((31,)),

time: 86.3 us -> 76.6 us (0.89)
  Pallas kernels: 76.1 us -> 65.7 us
    pallas_call x1, Pallas kernels: 65.6 us -> 54.3 us  [panel_factor(): pl.pallas_call(panel_kernel, out_shape=(jax.ShapeDtypeStruct((2 * PANEL,...]
    pallas_call x1, Pallas kernels: 10.5 us -> 11.5 us  [scenario_tiles(): pl.pallas_call(term_kernel, out_shape=(jax.ShapeDtypeStruct((tile_total,...]
where the time goes in v4:
time: 76.6 us; the launch traced here: 76 us
  Pallas kernels  65.7 us (86%)
  matrix products  8.33 us (11%)
  between operations  1.3 us (2%)
    pallas_call x1, Pallas kernels, panel_factor(): pl.pallas_call(panel_kernel, out_shape=(jax.ShapeDtypeStruct((2 * PANEL,...  54.3 us
    pallas_call x1, Pallas kernels, scenario_tiles(): pl.pallas_call(term_kernel, out_shape=(jax.ShapeDtypeStruct((tile_total,...  11.5 us
    dot_general x1, matrix products, direct(): lax.dot_general(own_rows, own_cols, (((1,), (1,)), ((), ())), preferred_e...  8.33 us

profile of v4, /device:TPU:7, one launch (start us, length us, event | category | flops | bytes accessed | tf_op | source)
XLA Modules:
  0.0 76.0 jit_solution(15210101916192330346)
XLA Ops:
  1.3 11.5 %scenario_tiles.1 = (f32[64,128,128]{2,1,0:T(8,128)}, f32[128,128]{1,0:T(8,128)}) custom-call(s32[1]{0:T(128)S(6)} %copy.8.panel_ref, s32[1,64]{1,0:T(1,128)} %mask_ref.1, bf16[1024,1024]{1,0:T(8,128)(2,1)} %bitcast.5, bf16[20,1024,128]{2,1,0:T(8,128)(2,1)} %bitcast.4, f32[1024,2048]{1,0:T(8,128)} %root_ref.1), custom_call_target="tpu_custom_call" | custom-call | tf_op jit(solution)/shard_map/scenario_tiles/pallas_call | solution.py:165
  12.8 54.3 %panel_factor.1 = (f32[256,128]{1,0:T(8,128)}, bf16[1024,128]{1,0:T(8,128)(2,1)}, bf16[2048,128]{1,0:T(8,128)(2,1)}) custom-call(s32[1]{0:T(128)S(6)} %copy.8.panel_ref, f32[64,128,128]{2,1,0:T(8,128)} %get-tuple-element.7.tiles_hbm, f32[128,128]{1,0:T(8,128)} %get-tuple-element.8.diag_in), custom_call_target="tpu_custom_call" | custom-call | tf_op jit(solution)/shard_map/panel_factor/pallas_call | solution.py:455
  67.0 0.0 copy-start
  67.0 8.3 %convolution_subtract_fusion = f32[1024,2048]{1,0:T(8,128)} fusion(f32[1024,2048]{1,0:T(8,128)} %root_ref.1, bf16[1024,128]{1,0:T(8,128)(2,1)} %get-tuple-element.9, bf16[2048,128]{1,0:T(8,128)(2,1)} %get-tuple-element.10), kind=kOutput, calls=%fused_computation | convolution fusion | flops 538968064 | bytes 17563648 | tf_op jit(solution)/shard_map/dot_general | solution.py:500
  75.4 0.0 copy-done
  75.4 0.7 copy.9
Async XLA Ops:
  67.0 8.3 %copy-start = (f32[256,128]{1,0:T(8,128)S(1)}, f32[256,128]{1,0:T(8,128)}, u32[]{:S(2)}) copy-start(f32[256,128]{1,0:T(8,128)} %get-tuple-element.15) | copy-start | bytes 393220

commit v5 on v4

--- a/solution.py
+++ b/solution.py
@@ -493,14 +493,35 @@
     )(panel_index, tiles, diag)
 
 
+def update_kernel(root_ref, rows_ref, cols_ref, out_ref):
+    out_ref[...] = root_ref[...] - lax.dot_general(
+        rows_ref[...], cols_ref[...], (((1,), (1,)), ((), ())), preferred_element_type=F32
+    )
+
+
+def trailing_update(root_matrix, own_rows, own_cols):
+    row_block, col_block = root_matrix.shape
+    step = PANEL
+    return pl.pallas_call(
+        update_kernel,
+        out_shape=jax.ShapeDtypeStruct(root_matrix.shape, F32),
+        grid=(row_block // step,),
+        in_specs=[
+            pl.BlockSpec((step, col_block), lambda i: (i, 0)),
+            pl.BlockSpec((step, PANEL), lambda i: (i, 0)),
+            pl.BlockSpec((col_block, PANEL), lambda i: (0, 0)),
+        ],
+        out_specs=pl.BlockSpec((step, col_block), lambda i: (i, 0)),
+        compiler_params=pltpu.CompilerParams(vmem_limit_bytes=32 * 2**20),
+        name="trailing_update",
+    )(root_matrix, own_rows, own_cols)
+
+
 def direct(root_matrix, inverse_block, link_tiles, tile_mask, panel_index):
     row_block, col_block = root_matrix.shape
     tiles, diag = scenario_tiles(root_matrix, inverse_block[0], link_tiles[0], tile_mask, panel_index)
     factor_rows, own_rows, own_cols = panel_factor(panel_index, tiles, diag, row_block, col_block)
-    update = lax.dot_general(
-        own_rows, own_cols, (((1,), (1,)), ((), ())), preferred_element_type=jnp.float32
-    )
-    return (root_matrix - update, factor_rows)
+    return (trailing_update(root_matrix, own_rows, own_cols), factor_rows)
 
 
 def solution(mesh):

time: 76.6 us -> 77.9 us (1.017); the launches traced: 76 us -> 78.2 us
  matrix products: 8.33 us -> 0 us
  local copies, waits for them, and re-layouts: 0.66 us -> 6.03 us
  Pallas kernels: 65.7 us -> 70.8 us
    dot_general x1 -> x0, matrix products: 8.33 us -> none  [direct(): lax.dot_general(own_rows, own_cols, (((1,), (1,)), ((), ())), preferred_e...]
    pallas_call x0 -> x1, Pallas kernels: none -> 5.42 us  [trailing_update(): pl.pallas_call(update_kernel, out_shape=jax.ShapeDtypeStruct(root_matrix....]
    unnamed x3 -> x9, local copies, waits for them, and re-layouts: 0.66 us -> 6.03 us
where the time goes in v5:
time: 77.9 us; the launch traced here: 78.2 us
  Pallas kernels  70.8 us (91%)
  local copies, waits for them, and re-layouts  6.03 us (8%)
  between operations  1.31 us (2%)
    pallas_call x1, Pallas kernels, panel_factor(): pl.pallas_call(panel_kernel, out_shape=(jax.ShapeDtypeStruct((2 * PANEL,...  54.1 us
    pallas_call x1, Pallas kernels, scenario_tiles(): pl.pallas_call(term_kernel, out_shape=(jax.ShapeDtypeStruct((tile_total,...  11.3 us
    unnamed x9, local copies, waits for them, and re-layouts  6.03 us
    pallas_call x1, Pallas kernels, trailing_update(): pl.pallas_call(update_kernel, out_shape=jax.ShapeDtypeStruct(root_matrix....  5.42 us

profile of v5, /device:TPU:7, one launch (start us, length us, event | category | flops | bytes accessed | tf_op | source)
XLA Modules:
  0.0 78.2 jit_solution(14857801681212725931)
XLA Ops:
  1.3 11.3 %scenario_tiles.1 = (f32[64,128,128]{2,1,0:T(8,128)}, f32[128,128]{1,0:T(8,128)}) custom-call(s32[1]{0:T(128)S(6)} %copy.8.panel_ref, s32[1,64]{1,0:T(1,128)} %mask_ref.1, bf16[1024,1024]{1,0:T(8,128)(2,1)} %bitcast.3, bf16[20,1024,128]{2,1,0:T(8,128)(2,1)} %bitcast.2, f32[1024,2048]{1,0:T(8,128)} %root_ref.3), custom_call_target="tpu_custom_call" | custom-call | tf_op jit(solution)/shard_map/scenario_tiles/pallas_call | solution.py:165
  12.6 54.1 %panel_factor.1 = (f32[256,128]{1,0:T(8,128)}, bf16[1024,128]{1,0:T(8,128)(2,1)}, bf16[2048,128]{1,0:T(8,128)(2,1)}) custom-call(s32[1]{0:T(128)S(6)} %copy.8.panel_ref, f32[64,128,128]{2,1,0:T(8,128)} %get-tuple-element.7.tiles_hbm, f32[128,128]{1,0:T(8,128)} %get-tuple-element.8.diag_in), custom_call_target="tpu_custom_call" | custom-call | tf_op jit(solution)/shard_map/panel_factor/pallas_call | solution.py:455
  66.7 0.0 copy-start
  66.7 3.4 %copy-done = f32[1024,2048]{1,0:T(8,128)S(1)} copy-done((f32[1024,2048]{1,0:T(8,128)S(1)}, f32[1024,2048]{1,0:T(8,128)}, u32[]{:S(2)}) %copy-start) | copy-done | bytes 8388632
  70.1 0.0 copy-start.1
  70.1 1.0 %copy-done.1 = bf16[2048,128]{1,0:T(8,128)(2,1)S(1)} copy-done((bf16[2048,128]{1,0:T(8,128)(2,1)S(1)}, bf16[2048,128]{1,0:T(8,128)(2,1)}, u32[]{:S(2)}) %copy-start.1) | copy-done | bytes 524312
  71.1 0.0 copy-start.2
  71.1 0.9 %copy-done.2 = bf16[1024,128]{1,0:T(8,128)(2,1)S(1)} copy-done((bf16[1024,128]{1,0:T(8,128)(2,1)S(1)}, bf16[1024,128]{1,0:T(8,128)(2,1)}, u32[]{:S(2)}) %copy-start.2) | copy-done | bytes 262168
  72.1 0.0 copy-start.3
  72.1 5.4 %trailing_update.1 = f32[1024,2048]{1,0:T(8,128)} custom-call(f32[1024,2048]{1,0:T(8,128)S(1)} %copy-done, bf16[1024,128]{1,0:T(8,128)(2,1)S(1)} %copy-done.2, bf16[2048,128]{1,0:T(8,128)(2,1)S(1)} %copy-done.1), custom_call_target="tpu_custom_call" | custom-call | tf_op jit(solution)/shard_map/trailing_update/pallas_call | solution.py:505
  77.5 0.0 copy-done.3
  77.5 0.7 copy.9
Async XLA Ops:
  66.7 3.4 %copy-start = (f32[1024,2048]{1,0:T(8,128)S(1)}, f32[1024,2048]{1,0:T(8,128)}, u32[]{:S(2)}) copy-start(f32[1024,2048]{1,0:T(8,128)} %root_ref.3) | copy-start | bytes 25165828
  70.1 1.0 %copy-start.1 = (bf16[2048,128]{1,0:T(8,128)(2,1)S(1)}, bf16[2048,128]{1,0:T(8,128)(2,1)}, u32[]{:S(2)}) copy-start(bf16[2048,128]{1,0:T(8,128)(2,1)} %get-tuple-element.10.cols_ref) | copy-start | bytes 1572868
  71.1 0.9 %copy-start.2 = (bf16[1024,128]{1,0:T(8,128)(2,1)S(1)}, bf16[1024,128]{1,0:T(8,128)(2,1)}, u32[]{:S(2)}) copy-start(bf16[1024,128]{1,0:T(8,128)(2,1)} %get-tuple-element.9.rows_ref) | copy-start | bytes 786436
  72.1 5.4 %copy-start.3 = (f32[256,128]{1,0:T(8,128)S(1)}, f32[256,128]{1,0:T(8,128)}, u32[]{:S(2)}) copy-start(f32[256,128]{1,0:T(8,128)} %get-tuple-element.15) | copy-start | bytes 393220
